TPU v7x, 32 devices: a whole 2x2x4 slice. The times are simulated.
32 devices in a mesh: row: 4 (over z), col: 8 (over y, x, core).
Axes of the slice: x: 2, y: 2, z: 4, core: 2. Of those that a mesh axis runs over, the one named last changes fastest.
Arguments:
- matrix_tiles: float32 [4, 8, 16, 512, 512], P('row', 'col'), may hold values from -0.25 to 0.25
- tile_rows: int32 [4, 8, 16], P('row', 'col'), may hold values from 0 to 63, as said below
- tile_columns: int32 [4, 8, 16], P('row', 'col'), may hold values from 0 to 31, as said below
- tile_counts: int32 [4, 8], P('row', 'col'), may hold values from 8 to 16, as said below
- primal_iter: float32 [2, 131072], P(None, ('col', 'row')), may hold values from -6 to 6
- dual_iter: float32 [2, 131072], P(None, ('row', 'col')), may hold values from -6 to 6
- requirement: float32 [131072], P('row'), may hold values from -68 to 68
- constraint_kind: int32 [131072], P('row'), may hold values from 0 to 1
- objective: float32 [131072], P('col'), may hold values from -68 to 68
- lower_bound: float32 [131072], P('col'), may hold values from -1.5 to 1.5
- upper_bound: float32 [131072], P('col'), may hold values from -1.5 to 1.5
- variable_kind: int32 [131072], P('col'), may hold values from 0 to 3
Outputs:
- primal_residual: float32 [2, 131072], P(None, ('row', 'col'))
- dual_residual: float32 [2, 131072], P(None, ('col', 'row'))
- metrics: float32 [2, 3], replicated
Inputs may be any that keep to these rules, and one draw needn't show every extreme that they name: `tile_counts`: slots below the count of a list hold live tiles, the others are padding; some list has all 16 slots live. `tile_rows`: in each constraint group, the first (8) slots of its lists name every block row of the group exactly once; later slots name any block row, and repeated tiles add. `tile_columns`: in each variable group, the first (8) slots of its lists name every block column of the group exactly once; later slots name any block column, and repeated tiles add. `constraint_kind`: 0 marks an equality, 1 a constraint of the form at least. `variable_kind`: 0 free, 1 lower bound only, 2 upper bound only, 3 both bounds.
All inputs are finite; a program needn't handle non-finite values.
Results may differ from a plain program's by a relative error of at most 0.0003.
Values sent between devices are 32-bit elements; how exact they have to be, the bound alone decides.
No kernel may reach another device: no remote copies, remote signals or barrier semaphores. Data moves between devices by JAX's collectives and lax.ppermute only.
A program may use at most 64 MiB of HBM per device.

v0:
```python
import jax
import jax.numpy as jnp
from jax import lax
from jax.sharding import PartitionSpec as P

HIGHEST_PRECISION = lax.Precision.HIGHEST


def primal_side(product, require_part, kind_part, dual_part):
    difference = require_part[None, :] - product
    residual = jnp.where(kind_part[None, :] == 1, jnp.maximum(difference, 0.0), difference)
    return (
        residual,
        jnp.sum(residual * residual, axis=1),
        jnp.sum(require_part * require_part),
        jnp.sum(require_part[None, :] * dual_part, axis=1),
    )


def dual_side(transposed, objective, lower_bound, upper_bound, variable_kind, primal_part):
    reduced = objective[None, :] - transposed
    lower_active = (variable_kind == 1) | (variable_kind == 3)
    upper_active = (variable_kind == 2) | (variable_kind == 3)
    multiplier = jnp.where(lower_active[None, :], jnp.maximum(reduced, 0.0), 0.0) + jnp.where(
        upper_active[None, :], jnp.minimum(reduced, 0.0), 0.0
    )
    residual = reduced - multiplier
    bound_sum = jnp.sum(
        lower_bound[None, :] * jnp.maximum(multiplier, 0.0)
        + upper_bound[None, :] * jnp.minimum(multiplier, 0.0),
        axis=1,
    )
    return (
        residual,
        jnp.sum(residual * residual, axis=1),
        jnp.sum(objective * objective),
        jnp.sum(objective[None, :] * primal_part, axis=1),
        bound_sum,
    )


def finish(
    primal_square,
    require_square,
    require_dot,
    dual_square,
    objective_square,
    objective_dot,
    bound_sum,
):
    primal_ratio = jnp.sqrt(primal_square) / (1.0 + jnp.sqrt(require_square))
    dual_ratio = jnp.sqrt(dual_square) / (1.0 + jnp.sqrt(objective_square))
    dual_value = require_dot + bound_sum
    duality_gap = jnp.abs(objective_dot - dual_value) / (
        1.0 + jnp.abs(objective_dot) + jnp.abs(dual_value)
    )
    return jnp.stack([primal_ratio, dual_ratio, duality_gap], axis=1)


def on_device(
    matrix_tiles,
    tile_rows,
    tile_columns,
    tile_counts,
    primal_iter,
    dual_iter,
    requirement,
    constraint_kind,
    objective,
    lower_bound,
    upper_bound,
    variable_kind,
):
    own_tiles = matrix_tiles[0, 0]
    slot_count = own_tiles.shape[0]
    block_size = own_tiles.shape[-1]
    candidates = primal_iter.shape[0]
    active = (lax.iota(jnp.int32, slot_count) < tile_counts[0, 0]).astype(jnp.float32)
    primal_group = lax.all_gather(primal_iter, "row", axis=1, tiled=True)
    dual_group = lax.all_gather(dual_iter, "col", axis=1, tiled=True)
    column_blocks = primal_group.shape[1] // block_size
    row_blocks = dual_group.shape[1] // block_size
    column_pick = (
        tile_columns[0, 0][:, None] == lax.iota(jnp.int32, column_blocks)[None, :]
    ).astype(jnp.float32)
    column_pick = column_pick * active[:, None]
    row_pick = (tile_rows[0, 0][:, None] == lax.iota(jnp.int32, row_blocks)[None, :]).astype(
        jnp.float32
    )
    row_pick = row_pick * active[:, None]
    primal_pick = jnp.einsum(
        "tc,scb->stb",
        column_pick,
        primal_group.reshape(candidates, column_blocks, block_size),
        precision=HIGHEST_PRECISION,
    )
    dual_pick = jnp.einsum(
        "tr,srb->stb",
        row_pick,
        dual_group.reshape(candidates, row_blocks, block_size),
        precision=HIGHEST_PRECISION,
    )
    tile_product = jnp.einsum("tij,stj->tsi", own_tiles, primal_pick, precision=HIGHEST_PRECISION)
    tile_transposed = jnp.einsum("tij,sti->tsj", own_tiles, dual_pick, precision=HIGHEST_PRECISION)
    row_share = dual_iter.shape[1]
    column_share = primal_iter.shape[1]
    row_start = lax.axis_index("col") * row_share
    column_start = lax.axis_index("row") * column_share
    product_part = jnp.einsum(
        "tr,tsi->sri", row_pick, tile_product, precision=HIGHEST_PRECISION
    ).reshape(candidates, row_blocks * block_size)
    transposed_part = jnp.einsum(
        "tc,tsj->scj", column_pick, tile_transposed, precision=HIGHEST_PRECISION
    ).reshape(candidates, column_blocks * block_size)
    product = lax.psum(product_part, "col")
    transposed = lax.psum(transposed_part, "row")
    primal_full, primal_square, require_square, require_dot = primal_side(
        product, requirement, constraint_kind, dual_group
    )
    primal_square, require_square, require_dot = lax.psum(
        (primal_square, require_square, require_dot), "row"
    )
    dual_full, dual_square, objective_square, objective_dot, bound_sum = dual_side(
        transposed, objective, lower_bound, upper_bound, variable_kind, primal_group
    )
    dual_square, objective_square, objective_dot, bound_sum = lax.psum(
        (dual_square, objective_square, objective_dot, bound_sum), "col"
    )
    primal_residual = lax.dynamic_slice_in_dim(primal_full, row_start, row_share, 1)
    dual_residual = lax.dynamic_slice_in_dim(dual_full, column_start, column_share, 1)
    metrics = finish(
        primal_square,
        require_square,
        require_dot,
        dual_square,
        objective_square,
        objective_dot,
        bound_sum,
    )
    return (primal_residual, dual_residual, metrics)


def solution(mesh):
    placed = (
        P("row", "col", None, None, None),
        P("row", "col", None),
        P("row", "col", None),
        P("row", "col"),
        P(None, ("col", "row")),
        P(None, ("row", "col")),
        P("row"),
        P("row"),
        P("col"),
        P("col"),
        P("col"),
        P("col"),
    )
    return jax.shard_map(
        on_device,
        mesh=mesh,
        in_specs=placed,
        out_specs=(P(None, ("row", "col")), P(None, ("col", "row")), P()),
        check_vma=False,
    )
```

profile of v0, /device:TPU:0, one launch (start us, length us, event | category | flops | bytes accessed | tf_op | source)
XLA Modules:
  0.0 147.8 jit_solution(15917342106605868104)
XLA Ops:
  7.2 0.0 all-reduce.7.cloned.1.call-start
  7.9 11.0 %all_gather.7 = f32[2,32768]{1,0:T(2,128)S(1)} all-gather(f32[2,4096]{1,0:T(2,128)} %param.17), channel_id=1, replica_groups=mesh['row'=4,'col'=8] {'col'}, dimensions={1}, use_global_device_ids=true | all-gather | bytes 294912 | tf_op jit(solution)/shard_map/all_gather | solution.py:80
  18.9 0.9 fusion.4
  19.8 0.0 copy-start.8
  19.8 0.0 copy-start.3
  19.9 0.0 copy-start.1
  19.9 0.0 copy-start.2
  19.9 0.0 copy-start
  19.9 0.0 copy-start.4
  19.9 0.0 copy-start.5
  19.9 11.6 %fusion = f32[16,2,512]{2,1,0:T(2,128)S(1)} fusion(f32[1,1,16,512,512]{4,3,2,1,0:T(8,128)} %param.12, f32[16,2,512]{2,0,1:T(8,128)S(1)} %fusion.4), kind=kOutput, calls=%fused_computation | convolution fusion | flops 100663296 | bytes 16908288 | tf_op jit(solution)/shard_map/tij,sti->tsj/dot_general | solution.py:104
  31.6 0.4 convolution_bitcast_fusion.1
  31.9 0.7 copy.23
  32.7 0.0 all-reduce.7.cloned.1.call-update
  32.7 0.0 all-reduce.5.cloned.1.call-start
  32.8 13.9 %all_gather.6 = f32[2,16384]{1,0:T(2,128)S(1)} all-gather(f32[2,4096]{1,0:T(2,128)S(1)} %copy-done.6), channel_id=1, replica_groups=mesh['row'=4,'col'=8] {'row'}, dimensions={1}, use_global_device_ids=true | all-gather | bytes 163840 | tf_op jit(solution)/shard_map/all_gather | solution.py:79
  46.7 0.3 fusion.7
  46.9 17.2 %fusion.2 = f32[16,2,512]{2,1,0:T(2,128)S(1)} fusion(f32[1,1,16,512,512]{4,3,2,1,0:T(8,128)} %param.12, f32[16,2,512]{2,0,1:T(8,128)S(1)} %fusion.7), kind=kOutput, calls=%fused_computation.2 | convolution fusion | flops 100663296 | bytes 16908288 | tf_op jit(solution)/shard_map/tij,stj->tsi/dot_general | solution.py:103
  64.1 0.5 convolution_bitcast_fusion
  64.6 0.9 copy.21
  65.5 0.0 all-reduce.5.cloned.1.call-update
  65.6 0.6 multiply_reduce_fusion.5
  66.3 0.6 multiply_reduce_fusion.4
  66.9 1.0 all-reduce.7.cloned.1.call-done
  67.9 1.5 add_reduce_fusion
  69.4 12.5 %all-reduce = (f32[2]{0:T(128)S(1)}, f32[2]{0:T(128)S(1)}, f32[2]{0:T(128)S(1)}, f32[]{:T(128)}) all-reduce(f32[2]{0:T(128)S(1)} %get-tuple-element.7, f32[2]{0:T(128)S(1)} %get-tuple-element.6, f32[2]{0:T(128)S(1)} %get-tuple-element.19, f32[]{:T(128)} %multiply_reduce_fusion.5), channel_id=1, replica_groups=mesh['row'=4,'col'=8] {'col'}, use_global_device_ids=true, to_apply=%region_11.12 | all-reduce | flops 7 | bytes 56 | tf_op jit(solution)/shard_map/psum | solution.py:126
  82.6 41.9 %all-reduce.5.cloned.1.call-done = f32[2,32768]{1,0:T(2,128)} async-done(((f32[2,32768]{1,0:T(2,128)}), f32[2,32768]{1,0:T(2,128)}) %all-reduce.5.cloned.1.call-update) | async-done | bytes 262160 | tf_op jit(solution)/shard_map/psum | solution.py:115
  124.5 1.5 %multiply_reduce_fusion.1 = (f32[2]{0:T(128)S(1)}, f32[2,32768]{1,0:T(2,128)S(1)}, f32[2]{0:T(128)S(1)}) fusion(f32[2,32768]{1,0:T(2,128)} %all-reduce.5.cloned.1.call-done, f32[32768]{0:T(1024)S(1)} %copy-done, pred[32768]{0:T(1024)(128)(4,1)S(1)} %broadcast_compare_fusion, f32[2,32768]{1,0:T(2,128)S(1)} %all_gather.7), kind=kLoop, calls=%fused_computation.11 | loop fusion | flops 458748 | bytes 950288 | tf_op jit(solution)/shard_map/reduce_sum | solution.py:14
  126.0 12.3 %all-reduce.1 = (f32[2]{0:T(128)S(1)}, f32[2]{0:T(128)S(1)}, f32[]{:T(128)}) all-reduce(f32[2]{0:T(128)S(1)} %get-tuple-element.21, f32[2]{0:T(128)S(1)} %get-tuple-element.15, f32[]{:T(128)} %multiply_reduce_fusion.4), channel_id=1, replica_groups=mesh['row'=4,'col'=8] {'row'}, use_global_device_ids=true, to_apply=%region_13.14 | all-reduce | flops 5 | bytes 40 | tf_op jit(solution)/shard_map/psum | solution.py:120
  139.1 0.6 copy.15
  139.8 0.6 constant_dynamic-slice_fusion
  140.4 0.6 constant_dynamic-slice_fusion.1
  (18 shorter events, 0.1 us)
Async XLA Ops:
  7.2 24.4 %copy-start.7 = (s32[1,1,16]{2,1,0:T(1,128)S(1)}, s32[1,1,16]{2,1,0:T(1,128)}, u32[]{:S(2)}) copy-start(s32[1,1,16]{2,1,0:T(1,128)} %param.14) | copy-start | bytes 196
  7.2 25.6 %copy-start.6 = (f32[2,4096]{1,0:T(2,128)S(1)}, f32[2,4096]{1,0:T(2,128)}, u32[]{:S(2)}) copy-start(f32[2,4096]{1,0:T(2,128)} %param.16) | copy-start | bytes 98308
  7.2 60.7 %all-reduce.7.cloned.1.call-start = ((), (), s32[]{:S(2)}) async-start(), calls=%async_computation.1 | async-start | bytes 262144 | tf_op jit(solution)/shard_map/psum | solution.py:116
  19.8 44.3 %copy-start.8 = (s32[1,1,16]{2,1,0:T(1,128)S(1)}, s32[1,1,16]{2,1,0:T(1,128)}, u32[]{:S(2)}) copy-start(s32[1,1,16]{2,1,0:T(1,128)} %param.13) | copy-start | bytes 196
  19.8 45.7 %copy-start.3 = (s32[16384]{0:T(1024)S(1)}, s32[16384]{0:T(1024)}, u32[]{:S(2)}) copy-start(s32[16384]{0:T(1024)} %param.23) | copy-start | bytes 196612
  19.9 45.8 %copy-start.1 = (f32[16384]{0:T(1024)S(1)}, f32[16384]{0:T(1024)}, u32[]{:S(2)}) copy-start(f32[16384]{0:T(1024)} %param.20) | copy-start | bytes 196612
  19.9 46.4 %copy-start.2 = (s32[32768]{0:T(1024)S(1)}, s32[32768]{0:T(1024)}, u32[]{:S(2)}) copy-start(s32[32768]{0:T(1024)} %param.19) | copy-start | bytes 393220
  19.9 46.4 %copy-start = (f32[32768]{0:T(1024)S(1)}, f32[32768]{0:T(1024)}, u32[]{:S(2)}) copy-start(f32[32768]{0:T(1024)} %param.18) | copy-start | bytes 393220
  19.9 48.0 %copy-start.4 = (f32[16384]{0:T(1024)S(1)}, f32[16384]{0:T(1024)}, u32[]{:S(2)}) copy-start(f32[16384]{0:T(1024)} %param.22) | copy-start | bytes 196612
  19.9 48.0 %copy-start.5 = (f32[16384]{0:T(1024)S(1)}, f32[16384]{0:T(1024)}, u32[]{:S(2)}) copy-start(f32[16384]{0:T(1024)} %param.21) | copy-start | bytes 196612
  32.7 91.8 %all-reduce.5.cloned.1.call-start = ((), (), s32[]{:S(2)}) async-start(), calls=%async_computation | async-start | bytes 524288 | tf_op jit(solution)/shard_map/psum | solution.py:115
Sparse Core Ops, SparseCore 0:
  32.8 35.0 all-reduce.6
  71.0 53.5 all-reduce.4
where the time goes:
time: 148 us
  blocking collectives  49.8 us (34%)
  waiting for transfers between devices  43 us (29%)
  matrix products  30.9 us (21%)
  between operations  16.3 us (11%)
  other arithmetic  4.29 us (3%)
  local copies, waits for them, and re-layouts  3.58 us (2%)
    psum x1, waiting for transfers between devices, on_device(): product = lax.psum(product_part, 'col')  41.9 us
    dot_general x1, matrix products, on_device(): jnp.einsum('tij,stj->tsi', own_tiles, primal_pick, precision=HIGHEST_PREC...  17.2 us
    all_gather x1, blocking collectives, on_device(): primal_group = lax.all_gather(primal_iter, 'row', axis=1, tiled=True)  13.9 us
    psum x1, blocking collectives, on_device(): lax.psum((dual_square, objective_square, objective_dot, bound_sum), 'col')  12.5 us
    psum x1, blocking collectives, on_device(): lax.psum((primal_square, require_square, require_dot), 'row')  12.3 us
    dot_general x1, matrix products, on_device(): jnp.einsum('tij,sti->tsj', own_tiles, dual_pick, precision=HIGHEST_PRECIS...  11.6 us
    all_gather x1, blocking collectives, on_device(): dual_group = lax.all_gather(dual_iter, 'col', axis=1, tiled=True)  11 us
  transfers between devices with their start and end apart: 2, of which 2 were waited for; matrix products, arithmetic and copies ran while one was open for 15% of the time, Pallas kernels for 0%

commit v1 on v0

v1 whole, which is shorter than its diff:
```python
import functools

import jax
import jax.numpy as jnp
from jax import lax
from jax.experimental import pallas as pl
from jax.experimental.pallas import tpu as pltpu
from jax.sharding import PartitionSpec as P

LANES = 128
SUB = 8
F32 = jnp.float32


def bits_of(count):
    return count.bit_length() - 1


def swap(value, axis, bit, count):
    return lax.ppermute(value, axis, [(i, i ^ bit) for i in range(count)])


def flip_bits(index, bits):
    out = jnp.int32(0)
    for bit in range(bits):
        out = out | (((index >> bit) & 1) << (bits - 1 - bit))
    return out


def tile_kernel(
    rows_ref,
    columns_ref,
    count_ref,
    primal_ref,
    dual_ref,
    tiles_ref,
    *refs,
    slot_count,
    block_size,
    row_devices,
    col_devices,
    row_share,
    column_share,
    extra_axes,
):
    extras = len(extra_axes)
    extra_in = refs[:extras]
    product_keep, product_send, transposed_keep, transposed_send = refs[extras : extras + 4]
    extra_out = refs[extras + 4 : 2 * extras + 4]
    tiles, product, transposed, tile_sems, extra_sems = refs[2 * extras + 4 :]
    my_row = lax.axis_index("row")
    my_col = lax.axis_index("col")
    live = count_ref[0, 0]

    def tile_copy(slot):
        return pltpu.make_async_copy(
            tiles_ref.at[0, 0, slot], tiles.at[slot], tile_sems.at[slot]
        )

    for slot in range(slot_count):

        @pl.when(slot < live)
        def _():
            tile_copy(slot).start()

    extra_copies = []
    for number, axis in enumerate(extra_axes):
        height = extra_out[number].shape[0]
        place = my_col if axis == "col" else my_row
        start = pl.multiple_of(place * height, SUB)
        extra_copies.append(
            pltpu.make_async_copy(
                extra_in[number].at[pl.ds(start, height)],
                extra_out[number],
                extra_sems.at[number],
            )
        )
        extra_copies[-1].start()

    product[...] = jnp.zeros(product.shape, F32)
    transposed[...] = jnp.zeros(transposed.shape, F32)
    chunks = block_size // LANES
    candidates = primal_ref.shape[1]
    row_blocks = row_share // block_size
    column_blocks = column_share // block_size

    def one_tile(slot, carry):
        tile_copy(slot).wait()
        block_row = rows_ref[0, 0, slot]
        block_column = columns_ref[0, 0, slot]
        row_owner = (block_row // row_blocks) ^ my_col
        column_owner = (block_column // column_blocks) ^ my_row
        row_inner = block_row % row_blocks
        column_inner = block_column % column_blocks
        primal = primal_ref[
            column_owner, :, pl.ds(pl.multiple_of(column_inner * block_size, LANES), block_size)
        ]
        dual = dual_ref[
            row_owner, :, pl.ds(pl.multiple_of(row_inner * block_size, LANES), block_size)
        ]
        spread = [
            [
                jnp.broadcast_to(primal[s : s + 1, k * LANES : (k + 1) * LANES], (SUB, LANES))
                for k in range(chunks)
            ]
            for s in range(candidates)
        ]
        dual_rows = jnp.concatenate([dual, jnp.zeros((SUB - candidates, block_size), F32)], 0)
        sums = [[jnp.zeros((SUB, LANES), F32) for _ in range(chunks)] for _ in range(candidates)]
        row_place = flip_bits(row_owner, bits_of(col_devices))
        column_place = flip_bits(column_owner, bits_of(row_devices))
        for band in range(chunks):
            dual_column = dual_rows[:, band * LANES : (band + 1) * LANES].T
            partial = [[] for _ in range(candidates)]
            for group in range(LANES // SUB):
                first = band * LANES + group * SUB
                part = [
                    tiles[slot, first : first + SUB, k * LANES : (k + 1) * LANES]
                    for k in range(chunks)
                ]
                for s in range(candidates):
                    weight = jnp.broadcast_to(
                        dual_column[group * SUB : (group + 1) * SUB, s : s + 1], (SUB, LANES)
                    )
                    total = part[0] * spread[s][0]
                    for k in range(1, chunks):
                        total = total + part[k] * spread[s][k]
                    partial[s].append(total)
                    for k in range(chunks):
                        sums[s][k] = sums[s][k] + part[k] * weight
            for s in range(candidates):
                turned = jnp.concatenate(partial[s], 0).T
                values = jnp.sum(turned, axis=0, keepdims=True)
                where = pl.ds(row_inner * chunks + band, 1)
                product[row_place, s, where, :] = product[row_place, s, where, :] + values
        for s in range(candidates):
            for k in range(chunks):
                values = jnp.sum(sums[s][k], axis=0, keepdims=True)
                where = pl.ds(column_inner * chunks + k, 1)
                transposed[column_place, s, where, :] = (
                    transposed[column_place, s, where, :] + values
                )
        return carry

    lax.fori_loop(0, live, one_tile, 0)
    half = col_devices // 2
    product_keep[...] = product[:half]
    product_send[...] = product[half:]
    half = row_devices // 2
    transposed_keep[...] = transposed[:half]
    transposed_send[...] = transposed[half:]
    for copy in extra_copies:
        copy.wait()


def side_kernel(
    product_keep,
    product_got,
    transposed_keep,
    transposed_got,
    require_ref,
    row_kind_ref,
    objective_ref,
    lower_ref,
    upper_ref,
    column_kind_ref,
    primal_ref,
    dual_ref,
    primal_out,
    dual_out,
    stats_out,
):
    candidates = primal_ref.shape[0]
    require = require_ref[...]
    row_kind = row_kind_ref[...]
    objective = objective_ref[...]
    lower = lower_ref[...]
    upper = upper_ref[...]
    column_kind = column_kind_ref[...]
    height = require.shape[0]
    width = objective.shape[0]

    def rows_of(ref, s, count):
        return jnp.concatenate(
            [ref[s : s + 1, k * LANES : (k + 1) * LANES] for k in range(count)], 0
        )

    def flat(value):
        return jnp.sum(value, axis=0, keepdims=True)

    lower_active = (column_kind == 1) | (column_kind == 3)
    upper_active = (column_kind == 2) | (column_kind == 3)
    stats = []
    for s in range(candidates):
        difference = require - (product_keep[0, s] + product_got[0, s])
        residual = jnp.where(row_kind == 1, jnp.maximum(difference, 0.0), difference)
        for k in range(height):
            primal_out[s : s + 1, k * LANES : (k + 1) * LANES] = residual[k : k + 1, :]
        reduced = objective - (transposed_keep[0, s] + transposed_got[0, s])
        multiplier = jnp.where(lower_active, jnp.maximum(reduced, 0.0), 0.0) + jnp.where(
            upper_active, jnp.minimum(reduced, 0.0), 0.0
        )
        dual_residual = reduced - multiplier
        for k in range(width):
            dual_out[s : s + 1, k * LANES : (k + 1) * LANES] = dual_residual[k : k + 1, :]
        stats += [
            flat(residual * residual),
            flat(dual_residual * dual_residual),
            flat(require * rows_of(dual_ref, s, height)),
            flat(objective * rows_of(primal_ref, s, width)),
            flat(lower * jnp.maximum(multiplier, 0.0) + upper * jnp.minimum(multiplier, 0.0)),
            flat(require * require),
            flat(objective * objective),
            jnp.zeros((1, LANES), F32),
        ]
    local = jnp.concatenate(stats, 0)
    for k in range(stats_out.shape[0]):
        stats_out[k] = local


def metric_kernel(stats_ref, out_ref):
    candidates = out_ref.shape[0]
    total = stats_ref[0]
    for k in range(1, stats_ref.shape[0]):
        total = total + stats_ref[k]
    total = jnp.broadcast_to(jnp.sum(total, axis=1, keepdims=True), total.shape)
    lines = []
    for s in range(candidates):
        line = [total[s * SUB + k : s * SUB + k + 1, :] for k in range(7)]
        primal_square, dual_square, require_dot, objective_dot, bound_sum = line[:5]
        require_square, objective_square = line[5:]
        dual_value = require_dot + bound_sum
        primal_ratio = jnp.sqrt(primal_square) / (1.0 + jnp.sqrt(require_square))
        dual_ratio = jnp.sqrt(dual_square) / (1.0 + jnp.sqrt(objective_square))
        gap = jnp.abs(objective_dot - dual_value) / (
            1.0 + jnp.abs(objective_dot) + jnp.abs(dual_value)
        )
        lane = lax.broadcasted_iota(jnp.int32, primal_ratio.shape, 1)
        lines.append(jnp.where(lane == 0, primal_ratio, jnp.where(lane == 1, dual_ratio, gap)))
    out_ref[...] = jnp.concatenate(lines, 0)[:, : out_ref.shape[1]]


def on_device(
    matrix_tiles,
    tile_rows,
    tile_columns,
    tile_counts,
    primal_iter,
    dual_iter,
    requirement,
    constraint_kind,
    objective,
    lower_bound,
    upper_bound,
    variable_kind,
    *,
    row_devices,
    col_devices,
):
    slot_count = matrix_tiles.shape[2]
    block_size = matrix_tiles.shape[-1]
    candidates, row_share = dual_iter.shape
    column_share = primal_iter.shape[1]
    primal_group = primal_iter[None]
    dual_group = dual_iter[None]
    for step in range(max(bits_of(row_devices), bits_of(col_devices))):
        bit = 1 << step
        primal_got = swap(primal_group, "row", bit, row_devices) if bit < row_devices else None
        dual_got = swap(dual_group, "col", bit, col_devices) if bit < col_devices else None
        if primal_got is not None:
            primal_group = jnp.concatenate([primal_group, primal_got], 0)
        if dual_got is not None:
            dual_group = jnp.concatenate([dual_group, dual_got], 0)

    extras = (
        (requirement, "col", row_share),
        (constraint_kind, "col", row_share),
        (objective, "row", column_share),
        (lower_bound, "row", column_share),
        (upper_bound, "row", column_share),
        (variable_kind, "row", column_share),
    )
    smem = pl.BlockSpec(memory_space=pltpu.SMEM)
    vmem = pl.BlockSpec(memory_space=pltpu.VMEM)
    hbm = pl.BlockSpec(memory_space=pl.ANY)
    row_height = row_share // LANES
    column_height = column_share // LANES
    product_shape = (col_devices, candidates, row_height, LANES)
    transposed_shape = (row_devices, candidates, column_height, LANES)

    def half_of(shape):
        return jax.ShapeDtypeStruct((shape[0] // 2,) + shape[1:], F32)

    outs = pl.pallas_call(
        functools.partial(
            tile_kernel,
            slot_count=slot_count,
            block_size=block_size,
            row_devices=row_devices,
            col_devices=col_devices,
            row_share=row_share,
            column_share=column_share,
            extra_axes=tuple(axis for _, axis, _ in extras),
        ),
        name="tile_pass",
        in_specs=[smem, smem, smem, vmem, vmem, hbm] + [hbm] * len(extras),
        out_specs=[vmem] * (4 + len(extras)),
        out_shape=[half_of(product_shape)] * 2
        + [half_of(transposed_shape)] * 2
        + [
            jax.ShapeDtypeStruct((share // LANES, LANES), value.dtype)
            for value, _, share in extras
        ],
        scratch_shapes=[
            pltpu.VMEM((slot_count, block_size, block_size), F32),
            pltpu.VMEM(product_shape, F32),
            pltpu.VMEM(transposed_shape, F32),
            pltpu.SemaphoreType.DMA((slot_count,)),
            pltpu.SemaphoreType.DMA((len(extras),)),
        ],
        compiler_params=pltpu.CompilerParams(vmem_limit_bytes=32 << 20),
    )(
        tile_rows,
        tile_columns,
        tile_counts,
        primal_group,
        dual_group,
        matrix_tiles,
        *[value.reshape(-1, LANES) for value, _, _ in extras],
    )
    product_keep, product_send, transposed_keep, transposed_send = outs[:4]
    for step in range(max(bits_of(row_devices), bits_of(col_devices))):
        bit = 1 << step
        product_got = swap(product_send, "col", bit, col_devices) if bit < col_devices else None
        transposed_got = (
            swap(transposed_send, "row", bit, row_devices) if bit < row_devices else None
        )
        if bit < col_devices:
            half = product_keep.shape[0] // 2
            if half:
                product_send = product_keep[half:] + product_got[half:]
                product_keep = product_keep[:half] + product_got[:half]
            else:
                product_last = product_got
        if bit < row_devices:
            half = transposed_keep.shape[0] // 2
            if half:
                transposed_send = transposed_keep[half:] + transposed_got[half:]
                transposed_keep = transposed_keep[:half] + transposed_got[:half]
            else:
                transposed_last = transposed_got

    devices = row_devices * col_devices
    stats_rows = candidates * SUB
    primal_residual, dual_residual, stats = pl.pallas_call(
        side_kernel,
        name="sides",
        in_specs=[vmem] * 12,
        out_specs=[vmem] * 3,
        out_shape=[
            jax.ShapeDtypeStruct(dual_iter.shape, F32),
            jax.ShapeDtypeStruct(primal_iter.shape, F32),
            jax.ShapeDtypeStruct((devices, stats_rows, LANES), F32),
        ],
    )(
        product_keep,
        product_last,
        transposed_keep,
        transposed_last,
        *outs[4:],
        primal_iter,
        dual_iter,
    )
    shared = lax.all_to_all(stats, ("row", "col"), 0, 0)
    metrics = pl.pallas_call(
        metric_kernel,
        name="metrics",
        in_specs=[vmem],
        out_specs=vmem,
        out_shape=jax.ShapeDtypeStruct((candidates, 3), F32),
    )(shared)
    return (primal_residual, dual_residual, metrics)


def solution(mesh):
    placed = (
        P("row", "col", None, None, None),
        P("row", "col", None),
        P("row", "col", None),
        P("row", "col"),
        P(None, ("col", "row")),
        P(None, ("row", "col")),
        P("row"),
        P("row"),
        P("col"),
        P("col"),
        P("col"),
        P("col"),
    )
    return jax.shard_map(
        functools.partial(
            on_device, row_devices=mesh.shape["row"], col_devices=mesh.shape["col"]
        ),
        mesh=mesh,
        in_specs=placed,
        out_specs=(P(None, ("row", "col")), P(None, ("col", "row")), P()),
        check_vma=False,
    )
```

time: 148 us -> 72.2 us (0.49)
  waiting for transfers between devices: 43 us -> 6.47 us
  blocking collectives: 49.8 us -> 13.8 us
  matrix products: 30.9 us -> 0 us
  starting transfers between devices: 0.08 us -> 17 us
  between operations: 16.3 us -> 1.42 us
  Pallas kernels: 0 us -> 14.5 us
  local copies, waits for them, and re-layouts: 3.58 us -> 12.9 us
    psum x2 -> x0, waiting for transfers between devices: 42.9 us -> none  [the longest x1 41.9 us: on_device(): product = lax.psum(product_part, 'col')]
    dot_general x6 -> x0, matrix products: 30.9 us -> none  [the longest x1 17.2 us: on_device(): jnp.einsum('tij,stj->tsi', own_tiles, primal_pick, precision=HIGHEST_PREC...]
    all_gather x2 -> x0, blocking collectives: 24.9 us -> none  [the longest x1 13.9 us: on_device(): primal_group = lax.all_gather(primal_iter, 'row', axis=1, tiled=True)]
    psum x2 -> x0, blocking collectives: 24.9 us -> none  [the longest x1 12.5 us: on_device(): lax.psum((dual_square, objective_square, objective_dot, bound_sum), 'col')]
    ppermute x0 -> x10, starting transfers between devices: none -> 17 us  [swap(): return lax.ppermute(value, axis, [(i, i ^ bit) for i in range(count)])]
    pallas_call x0 -> x3, Pallas kernels: none -> 14.5 us  [the longest x1 11.1 us: on_device(): pl.pallas_call(functools.partial(tile_kernel, slot_count=slot_count, bloc...]
    all_to_all x0 -> x1, blocking collectives: none -> 13.8 us  [on_device(): shared = lax.all_to_all(stats, ('row', 'col'), 0, 0)]
    unnamed x21 -> x34, local copies, waits for them, and re-layouts: 2.34 us -> 12.9 us
  transfers between devices with their start and end apart: 2 -> 10, of which waited for: 2 -> 5; matrix products, arithmetic and copies ran while one was open for 15% -> 6% of each run, Pallas kernels for 0% -> 0%
where the time goes in v1:
time: 72.2 us; the launch traced here: 71.4 us
  starting transfers between devices  17 us (24%)
  Pallas kernels  14.5 us (20%)
  blocking collectives  13.8 us (19%)
  local copies, waits for them, and re-layouts  12.9 us (18%)
  waiting for transfers between devices  6.47 us (9%)
  other arithmetic  5.33 us (7%)
  between operations  1.42 us (2%)
    ppermute x10, starting transfers between devices, swap(): return lax.ppermute(value, axis, [(i, i ^ bit) for i in range(count)])  17 us
    all_to_all x1, blocking collectives, on_device(): shared = lax.all_to_all(stats, ('row', 'col'), 0, 0)  13.8 us
    unnamed x34, local copies, waits for them, and re-layouts  12.9 us
    pallas_call x1, Pallas kernels, on_device(): pl.pallas_call(functools.partial(tile_kernel, slot_count=slot_count, bloc...  11.1 us
    ppermute x10, waiting for transfers between devices, swap(): return lax.ppermute(value, axis, [(i, i ^ bit) for i in range(count)])  6.47 us
    concatenate x3, other arithmetic, on_device(): dual_group = jnp.concatenate([dual_group, dual_got], 0)  2.49 us
    pallas_call x1, Pallas kernels, on_device(): pl.pallas_call(side_kernel, name='sides', in_specs=[vmem] * 12, out_specs...  1.72 us
    pallas_call x1, Pallas kernels, on_device(): pl.pallas_call(metric_kernel, name='metrics', in_specs=[vmem], out_specs=...  1.64 us
  transfers between devices with their start and end apart: 10, of which 5 were waited for; matrix products, arithmetic and copies ran while one was open for 6% of the time, Pallas kernels for 0%

profile of v1, /device:TPU:0, one launch (start us, length us, event | category | flops | bytes accessed | tf_op | source)
XLA Modules:
  0.0 71.4 jit_solution(5952874294998613375)
XLA Ops:
  1.2 2.6 %collective-permute-start = (f32[1,2,4096]{2,1,0:T(2,128)}, f32[1,2,4096]{2,1,0:T(2,128)S(1)}, u32[]{:S(2)}, u32[]{:S(2)}) collective-permute-start(f32[1,2,4096]{2,1,0:T(2,128)} %bitcast.18), channel_id=1, source_target_pairs={{0,8},{8,0},{16,24},{24,16},{1,9},{9,1},{17,25},{25,17},{2,10},{10... | collective-permute-start | bytes 98312 | tf_op jit(solution)/shard_map/ppermute | solution.py:20
  4.5 0.8 %pad_maximum_fusion.4 = f32[2,2,4096]{2,1,0:T(2,128)S(1)} fusion(f32[1,2,4096]{2,1,0:T(2,128)S(1)} %collective-permute-done.2, f32[1,2,4096]{2,1,0:T(2,128)} %bitcast.15), kind=kLoop, calls=%fused_computation.6 | loop fusion | flops 16384 | bytes 131072 | tf_op jit(solution)/shard_map/concatenate | solution.py:273
  5.3 1.6 %collective-permute-start.3 = (f32[2,2,4096]{2,1,0:T(2,128)S(1)}, f32[2,2,4096]{2,1,0:T(2,128)S(1)}, u32[]{:S(2)}, u32[]{:S(2)}) collective-permute-start(f32[2,2,4096]{2,1,0:T(2,128)S(1)} %pad_maximum_fusion.4), channel_id=1, source_target_pairs={{0,2},{1,3},{2,0},{3,1},{4,6},{5,7},{6,4},{7,5},{8,10},{9,11},{10,... | collective-permute-start | bytes 196616 | tf_op jit(solution)/shard_map/ppermute | solution.py:20
  6.8 0.8 %pad_maximum_fusion.3 = f32[2,2,4096]{2,1,0:T(2,128)S(1)} fusion(f32[1,2,4096]{2,1,0:T(2,128)S(1)} %collective-permute-done, f32[1,2,4096]{2,1,0:T(2,128)} %bitcast.19), kind=kLoop, calls=%fused_computation.5 | loop fusion | flops 16384 | bytes 131072 | tf_op jit(solution)/shard_map/concatenate | solution.py:271
  7.6 2.7 %collective-permute-start.1 = (f32[2,2,4096]{2,1,0:T(2,128)S(1)}, f32[2,2,4096]{2,1,0:T(2,128)S(1)}, u32[]{:S(2)}, u32[]{:S(2)}) collective-permute-start(f32[2,2,4096]{2,1,0:T(2,128)S(1)} %pad_maximum_fusion.3), channel_id=1, source_target_pairs={{0,16},{8,24},{16,0},{24,8},{1,17},{9,25},{17,1},{25,9},{2,18},{10... | collective-permute-start | bytes 196616 | tf_op jit(solution)/shard_map/ppermute | solution.py:20
  10.3 0.8 %pad_maximum_fusion.2 = f32[4,2,4096]{2,1,0:T(2,128)S(1)} fusion(f32[2,2,4096]{2,1,0:T(2,128)S(1)} %collective-permute-done.3, f32[1,2,4096]{2,1,0:T(2,128)S(1)} %collective-permute-done.2, f32[1,2,4096]{2,1,0:T(2,128)} %bitcast.16), kind=kLoop, calls=%fused_computation.2 | loop fusion | flops 65536 | bytes 262144 | tf_op jit(solution)/shard_map/concatenate | solution.py:273
  11.1 1.6 %collective-permute-start.4 = (f32[4,2,4096]{2,1,0:T(2,128)S(1)}, f32[4,2,4096]{2,1,0:T(2,128)S(1)}, u32[]{:S(2)}, u32[]{:S(2)}) collective-permute-start(f32[4,2,4096]{2,1,0:T(2,128)S(1)} %pad_maximum_fusion.2), channel_id=1, source_target_pairs={{0,4},{1,5},{2,6},{3,7},{4,0},{5,1},{6,2},{7,3},{8,12},{9,13},{10,... | collective-permute-start | bytes 393224 | tf_op jit(solution)/shard_map/ppermute | solution.py:20
  12.7 1.2 %collective-permute-done.1 = f32[2,2,4096]{2,1,0:T(2,128)S(1)} collective-permute-done((f32[2,2,4096]{2,1,0:T(2,128)S(1)}, f32[2,2,4096]{2,1,0:T(2,128)S(1)}, u32[]{:S(2)}, u32[]{:S(2)}) %collective-permute-start.1) | collective-permute-done | bytes 65568 | tf_op jit(solution)/shard_map/ppermute | solution.py:20
  13.9 0.8 %pad_maximum_fusion.1.primal_ref = f32[4,2,4096]{2,1,0:T(2,128)S(1)} fusion(f32[2,2,4096]{2,1,0:T(2,128)S(1)} %collective-permute-done.1, f32[1,2,4096]{2,1,0:T(2,128)S(1)} %collective-permute-done, f32[1,2,4096]{2,1,0:T(2,128)} %bitcast.20), kind=kLoop, calls=%fused_computation.1 | loop fusion | flops 65536 | bytes 262144 | tf_op jit(solution)/shard_map/concatenate | solution.py:271
  14.7 1.5 %collective-permute-done.4 = f32[4,2,4096]{2,1,0:T(2,128)S(1)} collective-permute-done((f32[4,2,4096]{2,1,0:T(2,128)S(1)}, f32[4,2,4096]{2,1,0:T(2,128)S(1)}, u32[]{:S(2)}, u32[]{:S(2)}) %collective-permute-start.4) | collective-permute-done | bytes 131104 | tf_op jit(solution)/shard_map/ppermute | solution.py:20
  16.2 0.9 %pad_maximum_fusion.dual_ref = f32[8,2,4096]{2,1,0:T(2,128)S(1)} fusion(f32[4,2,4096]{2,1,0:T(2,128)S(1)} %collective-permute-done.4, f32[2,2,4096]{2,1,0:T(2,128)S(1)} %collective-permute-done.3, f32[1,2,4096]{2,1,0:T(2,128)S(1)} %collective-permute-done.2, f32[1,2,4096]{2,1,0:T(2,128)} %bitcast.17), kind=kLoop, calls=%fused_computation | loop fusion | flops 196608 | bytes 524288 | tf_op jit(solution)/shard_map/concatenate | solution.py:273
  17.1 5.8 %copy-done = f32[1,1,16,512,512]{4,3,2,1,0:T(8,128)S(1)} copy-done((f32[1,1,16,512,512]{4,3,2,1,0:T(8,128)S(1)}, f32[1,1,16,512,512]{4,3,2,1,0:T(8,128)}, u32[]{:S(2)}) %copy-start) | copy-done | bytes 16777240
  22.8 0.9 %copy-done.1 = f32[32768]{0:T(1024)S(1)} copy-done((f32[32768]{0:T(1024)S(1)}, f32[32768]{0:T(1024)}, u32[]{:S(2)}) %copy-start.1) | copy-done | bytes 131096
  23.7 0.9 %copy-done.2 = s32[32768]{0:T(1024)S(1)} copy-done((s32[32768]{0:T(1024)S(1)}, s32[32768]{0:T(1024)}, u32[]{:S(2)}) %copy-start.2) | copy-done | bytes 131096
  24.6 0.8 %copy-done.3 = f32[16384]{0:T(1024)S(1)} copy-done((f32[16384]{0:T(1024)S(1)}, f32[16384]{0:T(1024)}, u32[]{:S(2)}) %copy-start.3) | copy-done | bytes 65560
  25.5 0.8 %copy-done.4 = f32[16384]{0:T(1024)S(1)} copy-done((f32[16384]{0:T(1024)S(1)}, f32[16384]{0:T(1024)}, u32[]{:S(2)}) %copy-start.4) | copy-done | bytes 65560
  26.3 0.8 %copy-done.5 = f32[16384]{0:T(1024)S(1)} copy-done((f32[16384]{0:T(1024)S(1)}, f32[16384]{0:T(1024)}, u32[]{:S(2)}) %copy-start.5) | copy-done | bytes 65560
  27.2 0.8 %copy-done.6 = s32[16384]{0:T(1024)S(1)} copy-done((s32[16384]{0:T(1024)S(1)}, s32[16384]{0:T(1024)}, u32[]{:S(2)}) %copy-start.6) | copy-done | bytes 65560
  28.0 0.7 copy-done.13
  28.7 0.7 copy-done.14
  29.3 11.1 %tile_pass.1 = (f32[4,2,32,128]{3,2,1,0:T(8,128)S(1)}, f32[4,2,32,128]{3,2,1,0:T(8,128)S(1)}, f32[2,2,32,128]{3,2,1,0:T(8,128)S(1)}, f32[2,2,32,128]{3,2,1,0:T(8...) custom-call(s32[1,1,16]{2,1,0:T(1,128)S(1)} %copy-done.13, ...), custom_call_target="tpu_custom_call" | custom-call | tf_op jit(solution)/shard_map/tile_pass/pallas_call | solution.py:294
  40.6 2.6 %collective-permute-start.8 = (f32[2,2,32,128]{3,2,1,0:T(8,128)S(1)}, f32[2,2,32,128]{3,2,1,0:T(8,128)S(1)}, u32[]{:S(2)}, u32[]{:S(2)}) collective-permute-start(f32[2,2,32,128]{3,2,1,0:T(8,128)S(1)} %get-tuple-element.19), channel_id=1, source_target_pairs={{0,8},{8,0},{16,24},{24,16},{1,9},{9,1},{17,25},{25,17},{2,10},{10... | collective-permute-start | bytes 196616 | tf_op jit(solution)/shard_map/ppermute | solution.py:20
  43.2 1.2 %collective-permute-start.6 = (f32[2,2,32,128]{3,2,1,0:T(8,128)S(1)}, f32[2,2,32,128]{3,2,1,0:T(8,128)S(1)}, u32[]{:S(2)}, u32[]{:S(2)}) collective-permute-start(f32[2,2,32,128]{3,2,1,0:T(8,128)S(1)} %get-tuple-element.30), channel_id=1, source_target_pairs={{0,2},{1,3},{2,0},{3,1},{4,6},{5,7},{6,4},{7,5},{8,10},{9,11},{10,... | collective-permute-start | bytes 196616 | tf_op jit(solution)/shard_map/ppermute | solution.py:20
  44.5 1.4 %collective-permute-done.8 = f32[2,2,32,128]{3,2,1,0:T(8,128)S(1)} collective-permute-done((f32[2,2,32,128]{3,2,1,0:T(8,128)S(1)}, f32[2,2,32,128]{3,2,1,0:T(8,128)S(1)}, u32[]{:S(2)}, u32[]{:S(2)}) %collective-permute-start.8) | collective-permute-done | bytes 65568 | tf_op jit(solution)/shard_map/ppermute | solution.py:20
  45.9 0.6 slice_add_fusion.2
  46.5 2.5 %collective-permute-start.9 = (f32[1,2,32,128]{3,2,1,0:T(8,128)S(1)}, f32[1,2,32,128]{3,2,1,0:T(8,128)S(1)}, u32[]{:S(2)}, u32[]{:S(2)}) collective-permute-start(f32[1,2,32,128]{3,2,1,0:T(8,128)S(1)} %get-tuple-element.31), channel_id=1, source_target_pairs={{0,16},{8,24},{16,0},{24,8},{1,17},{9,25},{17,1},{25,9},{2,18},{10... | collective-permute-start | bytes 98312 | tf_op jit(solution)/shard_map/ppermute | solution.py:20
  49.1 0.6 slice_add_fusion.4
  49.7 1.5 %collective-permute-start.7 = (f32[1,2,32,128]{3,2,1,0:T(8,128)S(1)}, f32[1,2,32,128]{3,2,1,0:T(8,128)S(1)}, u32[]{:S(2)}, u32[]{:S(2)}) collective-permute-start(f32[1,2,32,128]{3,2,1,0:T(8,128)S(1)} %get-tuple-element.33), channel_id=1, source_target_pairs={{0,4},{1,5},{2,6},{3,7},{4,0},{5,1},{6,2},{7,3},{8,12},{9,13},{10,... | collective-permute-start | bytes 98312 | tf_op jit(solution)/shard_map/ppermute | solution.py:20
  51.4 2.1 %collective-permute-done.7.product_got = f32[1,2,32,128]{3,2,1,0:T(8,128)S(1)} collective-permute-done((f32[1,2,32,128]{3,2,1,0:T(8,128)S(1)}, f32[1,2,32,128]{3,2,1,0:T(8,128)S(1)}, u32[]{:S(2)}, u32[]{:S(2)}) %collective-permute-start.7) | collective-permute-done | bytes 32800 | tf_op jit(solution)/shard_map/ppermute | solution.py:20
  54.2 1.7 %sides.1 = (f32[2,4096]{1,0:T(2,128)}, f32[2,4096]{1,0:T(2,128)}, f32[32,16,128]{2,1,0:T(8,128)}) custom-call(f32[1,2,32,128]{3,2,1,0:T(8,128)} %get-tuple-element.34.product_keep, f32[1,2,32,128]{3,2,1,0:T(8,128)} %copy-done.16, f32[1,2,32,128]{3,2,1,0:T(8,128)} %get-tuple-element.32.transposed_keep, f32[1,2,32,128]{3,2,1,0:T(8,128)} %copy-done.15, ...), custom_call_target="tpu_custom_call" | custom-call | tf_op jit(solution)/shard_map/sides/pallas_call | solution.py:355
  55.9 13.8 %all_to_all.5.stats_ref = f32[32,16,128]{2,1,0:T(8,128)} all-to-all(f32[32,16,128]{2,1,0:T(8,128)} %get-tuple-element.28), channel_id=1, replica_groups=mesh['row'=4,'col'=8] {'row','col'}, dimensions={0} | all-to-all | bytes 524288 | tf_op jit(solution)/shard_map/all_to_all | solution.py:374
  69.8 1.6 %metrics.1 = f32[2,3]{1,0:T(2,128)} custom-call(f32[32,16,128]{2,1,0:T(8,128)} %all_to_all.5.stats_ref), custom_call_target="tpu_custom_call" | custom-call | tf_op jit(solution)/shard_map/metrics/pallas_call | solution.py:375
  (34 shorter events, 1.6 us)
Async XLA Ops:
  0.6 3.9 %collective-permute-start.2 = (f32[1,2,4096]{2,1,0:T(2,128)}, f32[1,2,4096]{2,1,0:T(2,128)S(1)}, u32[]{:S(2)}, u32[]{:S(2)}) collective-permute-start(f32[1,2,4096]{2,1,0:T(2,128)} %bitcast.14), channel_id=1, source_target_pairs={{0,1},{1,0},{2,3},{3,2},{4,5},{5,4},{6,7},{7,6},{8,9},{9,8},{10,11... | collective-permute-start | bytes 98312 | tf_op jit(solution)/shard_map/ppermute | solution.py:20
  1.2 5.7 %collective-permute-start = (f32[1,2,4096]{2,1,0:T(2,128)}, f32[1,2,4096]{2,1,0:T(2,128)S(1)}, u32[]{:S(2)}, u32[]{:S(2)}) collective-permute-start(f32[1,2,4096]{2,1,0:T(2,128)} %bitcast.18), channel_id=1, source_target_pairs={{0,8},{8,0},{16,24},{24,16},{1,9},{9,1},{17,25},{25,17},{2,10},{10... | collective-permute-start | bytes 98312 | tf_op jit(solution)/shard_map/ppermute | solution.py:20
  5.3 5.0 %collective-permute-start.3 = (f32[2,2,4096]{2,1,0:T(2,128)S(1)}, f32[2,2,4096]{2,1,0:T(2,128)S(1)}, u32[]{:S(2)}, u32[]{:S(2)}) collective-permute-start(f32[2,2,4096]{2,1,0:T(2,128)S(1)} %pad_maximum_fusion.4), channel_id=1, source_target_pairs={{0,2},{1,3},{2,0},{3,1},{4,6},{5,7},{6,4},{7,5},{8,10},{9,11},{10,... | collective-permute-start | bytes 196616 | tf_op jit(solution)/shard_map/ppermute | solution.py:20
  7.6 6.2 %collective-permute-start.1 = (f32[2,2,4096]{2,1,0:T(2,128)S(1)}, f32[2,2,4096]{2,1,0:T(2,128)S(1)}, u32[]{:S(2)}, u32[]{:S(2)}) collective-permute-start(f32[2,2,4096]{2,1,0:T(2,128)S(1)} %pad_maximum_fusion.3), channel_id=1, source_target_pairs={{0,16},{8,24},{16,0},{24,8},{1,17},{9,25},{17,1},{25,9},{2,18},{10... | collective-permute-start | bytes 196616 | tf_op jit(solution)/shard_map/ppermute | solution.py:20
  11.1 5.1 %collective-permute-start.4 = (f32[4,2,4096]{2,1,0:T(2,128)S(1)}, f32[4,2,4096]{2,1,0:T(2,128)S(1)}, u32[]{:S(2)}, u32[]{:S(2)}) collective-permute-start(f32[4,2,4096]{2,1,0:T(2,128)S(1)} %pad_maximum_fusion.2), channel_id=1, source_target_pairs={{0,4},{1,5},{2,6},{3,7},{4,0},{5,1},{6,2},{7,3},{8,12},{9,13},{10,... | collective-permute-start | bytes 393224 | tf_op jit(solution)/shard_map/ppermute | solution.py:20
  17.1 5.8 %copy-start = (f32[1,1,16,512,512]{4,3,2,1,0:T(8,128)S(1)}, f32[1,1,16,512,512]{4,3,2,1,0:T(8,128)}, u32[]{:S(2)}) copy-start(f32[1,1,16,512,512]{4,3,2,1,0:T(8,128)} %tiles_ref.1) | copy-start | bytes 50331652
  22.8 0.9 %copy-start.1 = (f32[32768]{0:T(1024)S(1)}, f32[32768]{0:T(1024)}, u32[]{:S(2)}) copy-start(f32[32768]{0:T(1024)} %param.18) | copy-start | bytes 393220
  23.7 0.9 %copy-start.2 = (s32[32768]{0:T(1024)S(1)}, s32[32768]{0:T(1024)}, u32[]{:S(2)}) copy-start(s32[32768]{0:T(1024)} %param.19) | copy-start | bytes 393220
  24.6 0.8 %copy-start.3 = (f32[16384]{0:T(1024)S(1)}, f32[16384]{0:T(1024)}, u32[]{:S(2)}) copy-start(f32[16384]{0:T(1024)} %param.20) | copy-start | bytes 196612
  25.5 0.8 %copy-start.4 = (f32[16384]{0:T(1024)S(1)}, f32[16384]{0:T(1024)}, u32[]{:S(2)}) copy-start(f32[16384]{0:T(1024)} %param.21) | copy-start | bytes 196612
  26.3 0.8 %copy-start.5 = (f32[16384]{0:T(1024)S(1)}, f32[16384]{0:T(1024)}, u32[]{:S(2)}) copy-start(f32[16384]{0:T(1024)} %param.22) | copy-start | bytes 196612
  27.2 0.8 %copy-start.6 = (s32[16384]{0:T(1024)S(1)}, s32[16384]{0:T(1024)}, u32[]{:S(2)}) copy-start(s32[16384]{0:T(1024)} %param.23) | copy-start | bytes 196612
  28.0 0.7 copy-start.13
  28.7 0.7 copy-start.14
  40.5 6.0 %copy-start.7 = (f32[32,128]{1,0:T(8,128)}, f32[32,128]{1,0:T(8,128)S(1)}, u32[]{:S(2)}) copy-start(f32[32,128]{1,0:T(8,128)S(1)} %get-tuple-element.20.require_ref) | copy-start | bytes 49156
  40.5 6.0 %copy-start.8 = (s32[32,128]{1,0:T(8,128)}, s32[32,128]{1,0:T(8,128)S(1)}, u32[]{:S(2)}) copy-start(s32[32,128]{1,0:T(8,128)S(1)} %get-tuple-element.21.row_kind_ref) | copy-start | bytes 49156
  40.5 8.6 %copy-start.9 = (f32[32,128]{1,0:T(8,128)}, f32[32,128]{1,0:T(8,128)S(1)}, u32[]{:S(2)}) copy-start(f32[32,128]{1,0:T(8,128)S(1)} %get-tuple-element.22.objective_ref) | copy-start | bytes 49156
  40.5 8.6 %copy-start.10 = (f32[32,128]{1,0:T(8,128)}, f32[32,128]{1,0:T(8,128)S(1)}, u32[]{:S(2)}) copy-start(f32[32,128]{1,0:T(8,128)S(1)} %get-tuple-element.23.lower_ref) | copy-start | bytes 49156
  40.5 8.6 %copy-start.11 = (f32[32,128]{1,0:T(8,128)}, f32[32,128]{1,0:T(8,128)S(1)}, u32[]{:S(2)}) copy-start(f32[32,128]{1,0:T(8,128)S(1)} %get-tuple-element.24.upper_ref) | copy-start | bytes 49156
  40.5 9.2 %copy-start.12 = (s32[32,128]{1,0:T(8,128)}, s32[32,128]{1,0:T(8,128)S(1)}, u32[]{:S(2)}) copy-start(s32[32,128]{1,0:T(8,128)S(1)} %get-tuple-element.25.column_kind_ref) | copy-start | bytes 49156
  40.5 2.7 %collective-permute-start.5 = (f32[4,2,32,128]{3,2,1,0:T(8,128)S(1)}, f32[4,2,32,128]{3,2,1,0:T(8,128)S(1)}, u32[]{:S(2)}, u32[]{:S(2)}) collective-permute-start(f32[4,2,32,128]{3,2,1,0:T(8,128)S(1)} %get-tuple-element.17), channel_id=1, source_target_pairs={{0,1},{1,0},{2,3},{3,2},{4,5},{5,4},{6,7},{7,6},{8,9},{9,8},{10,11... | collective-permute-start | bytes 393224 | tf_op jit(solution)/shard_map/ppermute | solution.py:20
  40.6 5.3 %collective-permute-start.8 = (f32[2,2,32,128]{3,2,1,0:T(8,128)S(1)}, f32[2,2,32,128]{3,2,1,0:T(8,128)S(1)}, u32[]{:S(2)}, u32[]{:S(2)}) collective-permute-start(f32[2,2,32,128]{3,2,1,0:T(8,128)S(1)} %get-tuple-element.19), channel_id=1, source_target_pairs={{0,8},{8,0},{16,24},{24,16},{1,9},{9,1},{17,25},{25,17},{2,10},{10... | collective-permute-start | bytes 196616 | tf_op jit(solution)/shard_map/ppermute | solution.py:20
  43.2 5.8 %collective-permute-start.6 = (f32[2,2,32,128]{3,2,1,0:T(8,128)S(1)}, f32[2,2,32,128]{3,2,1,0:T(8,128)S(1)}, u32[]{:S(2)}, u32[]{:S(2)}) collective-permute-start(f32[2,2,32,128]{3,2,1,0:T(8,128)S(1)} %get-tuple-element.30), channel_id=1, source_target_pairs={{0,2},{1,3},{2,0},{3,1},{4,6},{5,7},{6,4},{7,5},{8,10},{9,11},{10,... | collective-permute-start | bytes 196616 | tf_op jit(solution)/shard_map/ppermute | solution.py:20
  46.5 4.9 %collective-permute-start.9 = (f32[1,2,32,128]{3,2,1,0:T(8,128)S(1)}, f32[1,2,32,128]{3,2,1,0:T(8,128)S(1)}, u32[]{:S(2)}, u32[]{:S(2)}) collective-permute-start(f32[1,2,32,128]{3,2,1,0:T(8,128)S(1)} %get-tuple-element.31), channel_id=1, source_target_pairs={{0,16},{8,24},{16,0},{24,8},{1,17},{9,25},{17,1},{25,9},{2,18},{10... | collective-permute-start | bytes 98312 | tf_op jit(solution)/shard_map/ppermute | solution.py:20
  49.7 3.9 %collective-permute-start.7 = (f32[1,2,32,128]{3,2,1,0:T(8,128)S(1)}, f32[1,2,32,128]{3,2,1,0:T(8,128)S(1)}, u32[]{:S(2)}, u32[]{:S(2)}) collective-permute-start(f32[1,2,32,128]{3,2,1,0:T(8,128)S(1)} %get-tuple-element.33), channel_id=1, source_target_pairs={{0,4},{1,5},{2,6},{3,7},{4,0},{5,1},{6,2},{7,3},{8,12},{9,13},{10,... | collective-permute-start | bytes 98312 | tf_op jit(solution)/shard_map/ppermute | solution.py:20
  51.4 2.2 %copy-start.15 = (f32[1,2,32,128]{3,2,1,0:T(8,128)}, f32[1,2,32,128]{3,2,1,0:T(8,128)S(1)}, u32[]{:S(2)}) copy-start(f32[1,2,32,128]{3,2,1,0:T(8,128)S(1)} %collective-permute-done.9.transposed_got) | copy-start | bytes 98308
  53.6 0.6 copy-start.16

commit v2 on v1

--- a/solution.py
+++ b/solution.py
@@ -20,9 +20,25 @@
     return lax.ppermute(value, axis, [(i, i ^ bit) for i in range(count)])
 
 
-def flip_bits(index, bits):
-    out = jnp.int32(0)
-    for bit in range(bits):
+def in_hbm(value):
+    return pltpu.with_memory_space_constraint(value, pltpu.HBM)
+
+
+def crossed(count):
+    return [bit | 1 for bit in plain(count)]
+
+
+def plain(count):
+    return [1 << step for step in range(bits_of(count))]
+
+
+def place_of(index, bits, cross):
+    low = index & 1
+    if cross:
+        for bit in range(1, bits):
+            low = low ^ ((index >> bit) & 1)
+    out = low << (bits - 1)
+    for bit in range(1, bits):
         out = out | (((index >> bit) & 1) << (bits - 1 - bit))
     return out
 
@@ -31,8 +47,6 @@
     rows_ref,
     columns_ref,
     count_ref,
-    primal_ref,
-    dual_ref,
     tiles_ref,
     *refs,
     slot_count,
@@ -44,10 +58,12 @@
     extra_axes,
 ):
     extras = len(extra_axes)
-    extra_in = refs[:extras]
-    product_keep, product_send, transposed_keep, transposed_send = refs[extras : extras + 4]
-    extra_out = refs[extras + 4 : 2 * extras + 4]
-    tiles, product, transposed, tile_sems, extra_sems = refs[2 * extras + 4 :]
+    primal_pieces, refs = refs[:row_devices], refs[row_devices:]
+    dual_pieces, refs = refs[:col_devices], refs[col_devices:]
+    extra_in, refs = refs[:extras], refs[extras:]
+    product_keep, product_send, transposed_keep, transposed_send = refs[:4]
+    extra_out, refs = refs[4 : extras + 4], refs[extras + 4 :]
+    tiles, primal_ref, dual_ref, product, transposed, tile_sems, extra_sems = refs
     my_row = lax.axis_index("row")
     my_col = lax.axis_index("col")
     live = count_ref[0, 0]
@@ -77,6 +93,10 @@
         )
         extra_copies[-1].start()
 
+    for number, piece in enumerate(primal_pieces):
+        primal_ref[number] = piece[...]
+    for number, piece in enumerate(dual_pieces):
+        dual_ref[number] = piece[...]
     product[...] = jnp.zeros(product.shape, F32)
     transposed[...] = jnp.zeros(transposed.shape, F32)
     chunks = block_size // LANES
@@ -107,8 +127,8 @@
         ]
         dual_rows = jnp.concatenate([dual, jnp.zeros((SUB - candidates, block_size), F32)], 0)
         sums = [[jnp.zeros((SUB, LANES), F32) for _ in range(chunks)] for _ in range(candidates)]
-        row_place = flip_bits(row_owner, bits_of(col_devices))
-        column_place = flip_bits(column_owner, bits_of(row_devices))
+        row_place = place_of(row_owner, bits_of(col_devices), True)
+        column_place = place_of(column_owner, bits_of(row_devices), False)
         for band in range(chunks):
             dual_column = dual_rows[:, band * LANES : (band + 1) * LANES].T
             partial = [[] for _ in range(candidates)]
@@ -214,19 +234,22 @@
             jnp.zeros((1, LANES), F32),
         ]
     local = jnp.concatenate(stats, 0)
-    for k in range(stats_out.shape[0]):
-        stats_out[k] = local
+    local = jnp.broadcast_to(jnp.sum(local, axis=1, keepdims=True), local.shape)
+    line = lax.broadcasted_iota(jnp.int32, local.shape, 0)
+    lane = lax.broadcasted_iota(jnp.int32, local.shape, 1)
+    packed = jnp.sum(jnp.where(line == lane, local, 0.0), axis=0, keepdims=True)
+    stats_out[...] = jnp.broadcast_to(packed, stats_out.shape)
 
 
 def metric_kernel(stats_ref, out_ref):
     candidates = out_ref.shape[0]
-    total = stats_ref[0]
-    for k in range(1, stats_ref.shape[0]):
-        total = total + stats_ref[k]
-    total = jnp.broadcast_to(jnp.sum(total, axis=1, keepdims=True), total.shape)
+    total = jnp.sum(stats_ref[...], axis=0, keepdims=True)
     lines = []
     for s in range(candidates):
-        line = [total[s * SUB + k : s * SUB + k + 1, :] for k in range(7)]
+        line = [
+            jnp.broadcast_to(total[:, s * SUB + k : s * SUB + k + 1], total.shape)
+            for k in range(7)
+        ]
         primal_square, dual_square, require_dot, objective_dot, bound_sum = line[:5]
         require_square, objective_square = line[5:]
         dual_value = require_dot + bound_sum
@@ -261,16 +284,27 @@
     block_size = matrix_tiles.shape[-1]
     candidates, row_share = dual_iter.shape
     column_share = primal_iter.shape[1]
-    primal_group = primal_iter[None]
-    dual_group = dual_iter[None]
-    for step in range(max(bits_of(row_devices), bits_of(col_devices))):
-        bit = 1 << step
-        primal_got = swap(primal_group, "row", bit, row_devices) if bit < row_devices else None
-        dual_got = swap(dual_group, "col", bit, col_devices) if bit < col_devices else None
-        if primal_got is not None:
-            primal_group = jnp.concatenate([primal_group, primal_got], 0)
-        if dual_got is not None:
-            dual_group = jnp.concatenate([dual_group, dual_got], 0)
+    primal_pieces = {0: primal_iter}
+    dual_pieces = {0: dual_iter}
+    row_steps = plain(row_devices)
+    col_steps = crossed(col_devices)
+    for step in range(max(len(row_steps), len(col_steps))):
+        if step < len(row_steps):
+            bit = row_steps[step]
+            primal_pieces.update(
+                {
+                    rel ^ bit: swap(value, "row", bit, row_devices)
+                    for rel, value in primal_pieces.items()
+                }
+            )
+        if step < len(col_steps):
+            bit = (col_steps[1:] + col_steps[:1])[step]
+            dual_pieces.update(
+                {
+                    rel ^ bit: swap(value, "col", bit, col_devices)
+                    for rel, value in dual_pieces.items()
+                }
+            )
 
     extras = (
         (requirement, "col", row_share),
@@ -282,7 +316,7 @@
     )
     smem = pl.BlockSpec(memory_space=pltpu.SMEM)
     vmem = pl.BlockSpec(memory_space=pltpu.VMEM)
-    hbm = pl.BlockSpec(memory_space=pl.ANY)
+    hbm = pl.BlockSpec(memory_space=pltpu.HBM)
     row_height = row_share // LANES
     column_height = column_share // LANES
     product_shape = (col_devices, candidates, row_height, LANES)
@@ -303,7 +337,10 @@
             extra_axes=tuple(axis for _, axis, _ in extras),
         ),
         name="tile_pass",
-        in_specs=[smem, smem, smem, vmem, vmem, hbm] + [hbm] * len(extras),
+        in_specs=[smem] * 3
+        + [hbm]
+        + [vmem] * (row_devices + col_devices)
+        + [hbm] * len(extras),
         out_specs=[vmem] * (4 + len(extras)),
         out_shape=[half_of(product_shape)] * 2
         + [half_of(transposed_shape)] * 2
@@ -313,6 +350,8 @@
         ],
         scratch_shapes=[
             pltpu.VMEM((slot_count, block_size, block_size), F32),
+            pltpu.VMEM((row_devices, candidates, column_share), F32),
+            pltpu.VMEM((col_devices, candidates, row_share), F32),
             pltpu.VMEM(product_shape, F32),
             pltpu.VMEM(transposed_shape, F32),
             pltpu.SemaphoreType.DMA((slot_count,)),
@@ -320,38 +359,32 @@
         ],
         compiler_params=pltpu.CompilerParams(vmem_limit_bytes=32 << 20),
     )(
-        tile_rows,
-        tile_columns,
+        in_hbm(tile_rows),
+        in_hbm(tile_columns),
         tile_counts,
-        primal_group,
-        dual_group,
-        matrix_tiles,
-        *[value.reshape(-1, LANES) for value, _, _ in extras],
+        in_hbm(matrix_tiles),
+        in_hbm(primal_iter),
+        *[primal_pieces[rel] for rel in range(1, row_devices)],
+        in_hbm(dual_iter),
+        *[dual_pieces[rel] for rel in range(1, col_devices)],
+        *[in_hbm(value.reshape(-1, LANES)) for value, _, _ in extras],
     )
     product_keep, product_send, transposed_keep, transposed_send = outs[:4]
-    for step in range(max(bits_of(row_devices), bits_of(col_devices))):
-        bit = 1 << step
-        product_got = swap(product_send, "col", bit, col_devices) if bit < col_devices else None
-        transposed_got = (
-            swap(transposed_send, "row", bit, row_devices) if bit < row_devices else None
-        )
-        if bit < col_devices:
+    for step in range(max(len(row_steps), len(col_steps))):
+        if step < len(col_steps):
+            product_got = swap(product_send, "col", col_steps[step], col_devices)
+        if step < len(row_steps):
+            transposed_got = swap(transposed_send, "row", row_steps[step], row_devices)
+        if step + 1 < len(col_steps):
             half = product_keep.shape[0] // 2
-            if half:
-                product_send = product_keep[half:] + product_got[half:]
-                product_keep = product_keep[:half] + product_got[:half]
-            else:
-                product_last = product_got
-        if bit < row_devices:
+            product_send = product_keep[half:] + product_got[half:]
+            product_keep = product_keep[:half] + product_got[:half]
+        if step + 1 < len(row_steps):
             half = transposed_keep.shape[0] // 2
-            if half:
-                transposed_send = transposed_keep[half:] + transposed_got[half:]
-                transposed_keep = transposed_keep[:half] + transposed_got[:half]
-            else:
-                transposed_last = transposed_got
+            transposed_send = transposed_keep[half:] + transposed_got[half:]
+            transposed_keep = transposed_keep[:half] + transposed_got[:half]
 
     devices = row_devices * col_devices
-    stats_rows = candidates * SUB
     primal_residual, dual_residual, stats = pl.pallas_call(
         side_kernel,
         name="sides",
@@ -360,13 +393,14 @@
         out_shape=[
             jax.ShapeDtypeStruct(dual_iter.shape, F32),
             jax.ShapeDtypeStruct(primal_iter.shape, F32),
-            jax.ShapeDtypeStruct((devices, stats_rows, LANES), F32),
+            jax.ShapeDtypeStruct((devices, LANES), F32),
         ],
+        compiler_params=pltpu.CompilerParams(vmem_limit_bytes=8 << 20),
     )(
         product_keep,
-        product_last,
+        product_got,
         transposed_keep,
-        transposed_last,
+        transposed_got,
         *outs[4:],
         primal_iter,
         dual_iter,
@@ -378,6 +412,7 @@
         in_specs=[vmem],
         out_specs=vmem,
         out_shape=jax.ShapeDtypeStruct((candidates, 3), F32),
+        compiler_params=pltpu.CompilerParams(vmem_limit_bytes=8 << 20),
     )(shared)
     return (primal_residual, dual_residual, metrics)
 

time: 72.2 us -> 48.9 us (0.68)
  local copies, waits for them, and re-layouts: 12.9 us -> 0.01 us
  other arithmetic: 5.33 us -> 0.04 us
  starting transfers between devices: 17 us -> 11.8 us
  waiting for transfers between devices: 6.47 us -> 10.9 us
  blocking collectives: 13.8 us -> 10.2 us
    unnamed x34 -> x4, local copies, waits for them, and re-layouts: 12.9 us -> 0.01 us
    ppermute x10 -> x15, starting transfers between devices: 17 us -> 11.8 us  [swap(): return lax.ppermute(value, axis, [(i, i ^ bit) for i in range(count)])]
    ppermute x10 -> x15, waiting for transfers between devices: 6.47 us -> 10.9 us  [swap(): return lax.ppermute(value, axis, [(i, i ^ bit) for i in range(count)])]
    concatenate x5 -> x0, other arithmetic: 4.09 us -> none  [the longest x3 2.49 us: on_device(): dual_group = jnp.concatenate([dual_group, dual_got], 0)]
    all_to_all x1, blocking collectives: 13.8 us -> 10.2 us  [on_device(): shared = lax.all_to_all(stats, ('row', 'col'), 0, 0)]
    pallas_call x1, Pallas kernels: 11.1 us -> 12.7 us  [on_device(): pl.pallas_call(functools.partial(tile_kernel, slot_count=slot_count, bloc...]
    pallas_call x1, Pallas kernels: 1.72 us -> 0.72 us  [on_device(): pl.pallas_call(side_kernel, name='sides', in_specs=[vmem] * 12, out_specs...]
    pallas_call x1, Pallas kernels: 1.64 us -> 0.67 us  [on_device(): pl.pallas_call(metric_kernel, name='metrics', in_specs=[vmem], out_specs=...]
  transfers between devices with their start and end apart: 10 -> 15, of which waited for: 5 -> 7; matrix products, arithmetic and copies ran while one was open for 6% -> 0% of each run, Pallas kernels for 0% -> 0%
where the time goes in v2:
time: 48.9 us; the launch traced here: 48.4 us
  Pallas kernels  14.1 us (29%)
  starting transfers between devices  11.8 us (24%)
  waiting for transfers between devices  10.9 us (22%)
  blocking collectives  10.2 us (21%)
  between operations  1.38 us (3%)
    pallas_call x1, Pallas kernels, on_device(): pl.pallas_call(functools.partial(tile_kernel, slot_count=slot_count, bloc...  12.7 us
    ppermute x15, starting transfers between devices, swap(): return lax.ppermute(value, axis, [(i, i ^ bit) for i in range(count)])  11.8 us
    ppermute x15, waiting for transfers between devices, swap(): return lax.ppermute(value, axis, [(i, i ^ bit) for i in range(count)])  10.9 us
    all_to_all x1, blocking collectives, on_device(): shared = lax.all_to_all(stats, ('row', 'col'), 0, 0)  10.2 us
  transfers between devices with their start and end apart: 15, of which 7 were waited for; matrix products, arithmetic and copies ran while one was open for 0% of the time, Pallas kernels for 0%

profile of v2, /device:TPU:0, one launch (start us, length us, event | category | flops | bytes accessed | tf_op | source)
XLA Modules:
  0.0 48.4 jit_solution(18424811585756633454)
XLA Ops:
  0.7 2.5 %collective-permute-start.4 = (f32[2,4096]{1,0:T(2,128)}, f32[2,4096]{1,0:T(2,128)S(1)}, u32[]{:S(2)}, u32[]{:S(2)}) collective-permute-start(f32[2,4096]{1,0:T(2,128)} %dual_ref.1), channel_id=1, source_target_pairs={{0,3},{1,2},{2,1},{3,0},{4,7},{5,6},{6,5},{7,4},{8,11},{9,10},{10,... | collective-permute-start | bytes 98312 | tf_op jit(solution)/shard_map/ppermute | solution.py:20
  3.1 2.6 %collective-permute-start.1 = (f32[2,4096]{1,0:T(2,128)}, f32[2,4096]{1,0:T(2,128)S(1)}, u32[]{:S(2)}, u32[]{:S(2)}) collective-permute-start(f32[2,4096]{1,0:T(2,128)} %primal_ref.1), channel_id=1, source_target_pairs={{0,16},{8,24},{16,0},{24,8},{1,17},{9,25},{17,1},{25,9},{2,18},{10... | collective-permute-start | bytes 98312 | tf_op jit(solution)/shard_map/ppermute | solution.py:20
  5.7 1.6 %collective-permute-start = (f32[2,4096]{1,0:T(2,128)}, f32[2,4096]{1,0:T(2,128)S(1)}, u32[]{:S(2)}, u32[]{:S(2)}) collective-permute-start(f32[2,4096]{1,0:T(2,128)} %primal_ref.1), channel_id=1, source_target_pairs={{0,8},{8,0},{16,24},{24,16},{1,9},{9,1},{17,25},{25,17},{2,10},{10... | collective-permute-start | bytes 98312 | tf_op jit(solution)/shard_map/ppermute | solution.py:20
  7.3 1.2 %collective-permute-start.6 = (f32[2,4096]{1,0:T(2,128)}, f32[2,4096]{1,0:T(2,128)S(1)}, u32[]{:S(2)}, u32[]{:S(2)}) collective-permute-start(f32[2,4096]{1,0:T(2,128)} %dual_ref.1), channel_id=1, source_target_pairs={{0,5},{1,4},{2,7},{3,6},{4,1},{5,0},{6,3},{7,2},{8,13},{9,12},{10,... | collective-permute-start | bytes 98312 | tf_op jit(solution)/shard_map/ppermute | solution.py:20
  8.5 0.5 %collective-permute-start.8 = (f32[2,4096]{1,0:T(2,128)S(1)}, f32[2,4096]{1,0:T(2,128)S(1)}, u32[]{:S(2)}, u32[]{:S(2)}) collective-permute-start(f32[2,4096]{1,0:T(2,128)S(1)} %collective-permute-done.4.refs_7_), channel_id=1, source_target_pairs={{0,5},{1,4},{2,7},{3,6},{4,1},{5,0},{6,3},{7,2},{8,13},{9,12},{10,... | collective-permute-start | bytes 98312 | tf_op jit(solution)/shard_map/ppermute | solution.py:20
  9.0 0.1 collective-permute-start.3
  9.2 0.4 collective-permute-start.5
  9.6 0.3 collective-permute-done.refs_1_
  9.8 1.0 %collective-permute-start.2 = (f32[2,4096]{1,0:T(2,128)S(1)}, f32[2,4096]{1,0:T(2,128)S(1)}, u32[]{:S(2)}, u32[]{:S(2)}) collective-permute-start(f32[2,4096]{1,0:T(2,128)S(1)} %collective-permute-done.refs_1_), channel_id=1, source_target_pairs={{0,16},{8,24},{16,0},{24,8},{1,17},{9,25},{17,1},{25,9},{2,18},{10... | collective-permute-start | bytes 98312 | tf_op jit(solution)/shard_map/ppermute | solution.py:20
  10.9 0.0 collective-permute-done.6.refs_9_
  10.9 0.2 collective-permute-start.7
  11.1 0.8 %collective-permute-done.8.refs_10_ = f32[2,4096]{1,0:T(2,128)S(1)} collective-permute-done((f32[2,4096]{1,0:T(2,128)S(1)}, f32[2,4096]{1,0:T(2,128)S(1)}, u32[]{:S(2)}, u32[]{:S(2)}) %collective-permute-start.8) | collective-permute-done | bytes 32800 | tf_op jit(solution)/shard_map/ppermute | solution.py:20
  11.9 0.4 collective-permute-start.9
  12.9 0.0 collective-permute-done.3.refs_5_
  12.9 1.7 %collective-permute-done.2.refs_3_ = f32[2,4096]{1,0:T(2,128)S(1)} collective-permute-done((f32[2,4096]{1,0:T(2,128)S(1)}, f32[2,4096]{1,0:T(2,128)S(1)}, u32[]{:S(2)}, u32[]{:S(2)}) %collective-permute-start.2) | collective-permute-done | bytes 32800 | tf_op jit(solution)/shard_map/ppermute | solution.py:20
  14.7 0.0 collective-permute-done.7.refs_8_
  14.7 0.0 collective-permute-done.5.refs_6_
  14.7 0.0 collective-permute-done.9.refs_11_
  14.7 12.7 %tile_pass.1 = (f32[4,2,32,128]{3,2,1,0:T(8,128)S(1)}, f32[4,2,32,128]{3,2,1,0:T(8,128)S(1)}, f32[2,2,32,128]{3,2,1,0:T(8,128)S(1)}, f32[2,2,32,128]{3,2,1,0:T(8...) custom-call(s32[1,1,16]{2,1,0:T(1,128)} %rows_ref.1, ...), custom_call_target="tpu_custom_call" | custom-call | tf_op jit(solution)/shard_map/tile_pass/pallas_call | solution.py:328
  27.4 0.1 collective-permute-start.10
  27.4 1.0 %collective-permute-start.13 = (f32[2,2,32,128]{3,2,1,0:T(8,128)S(1)}, f32[2,2,32,128]{3,2,1,0:T(8,128)S(1)}, u32[]{:S(2)}, u32[]{:S(2)}) collective-permute-start(f32[2,2,32,128]{3,2,1,0:T(8,128)S(1)} %get-tuple-element.19), channel_id=1, source_target_pairs={{0,8},{8,0},{16,24},{24,16},{1,9},{9,1},{17,25},{25,17},{2,10},{10... | collective-permute-start | bytes 196616 | tf_op jit(solution)/shard_map/ppermute | solution.py:20
  28.4 0.3 collective-permute-done.10
  28.8 0.1 collective-permute-start.11
  28.9 3.1 %collective-permute-done.13 = f32[2,2,32,128]{3,2,1,0:T(8,128)S(1)} collective-permute-done((f32[2,2,32,128]{3,2,1,0:T(8,128)S(1)}, f32[2,2,32,128]{3,2,1,0:T(8,128)S(1)}, u32[]{:S(2)}, u32[]{:S(2)}) %collective-permute-start.13) | collective-permute-done | bytes 65568 | tf_op jit(solution)/shard_map/ppermute | solution.py:20
  31.9 0.1 collective-permute-start.14
  32.0 0.9 %collective-permute-done.11 = f32[2,2,32,128]{3,2,1,0:T(8,128)S(1)} collective-permute-done((f32[2,2,32,128]{3,2,1,0:T(8,128)S(1)}, f32[2,2,32,128]{3,2,1,0:T(8,128)S(1)}, u32[]{:S(2)}, u32[]{:S(2)}) %collective-permute-start.11) | collective-permute-done | bytes 65568 | tf_op jit(solution)/shard_map/ppermute | solution.py:20
  32.9 0.1 collective-permute-start.12
  33.0 3.8 %collective-permute-done.14.transposed_got = f32[1,2,32,128]{3,2,1,0:T(8,128)S(1)} collective-permute-done((f32[1,2,32,128]{3,2,1,0:T(8,128)S(1)}, f32[1,2,32,128]{3,2,1,0:T(8,128)S(1)}, u32[]{:S(2)}, u32[]{:S(2)}) %collective-permute-start.14) | collective-permute-done | bytes 32800 | tf_op jit(solution)/shard_map/ppermute | solution.py:20
  36.8 0.0 collective-permute-done.12.product_got
  36.8 0.7 %sides.1 = (f32[2,4096]{1,0:T(2,128)}, f32[2,4096]{1,0:T(2,128)}, f32[32,128]{1,0:T(8,128)S(1)}) custom-call(f32[1,2,32,128]{3,2,1,0:T(8,128)S(1)} %get-tuple-element.34.product_keep, f32[1,2,32,128]{3,2,1,0:T(8,128)S(1)} %collective-permute-done.12.product_got, f32[1,2,32,128]{3,2,1,0:T(8,128)S(1)} %get-tuple-element.32.transposed_keep, ...), custom_call_target="tpu_custom_call" | custom-call | tf_op jit(solution)/shard_map/sides/pallas_call | solution.py:388
  37.6 10.2 %all_to_all.11 = f32[32,1,128]{2,1,0:T(1,128)S(1)} all-to-all(f32[32,1,128]{2,1,0:T(1,128)S(1)} %bitcast.11), channel_id=1, replica_groups=mesh['row'=4,'col'=8] {'row','col'}, dimensions={0} | all-to-all | bytes 32768 | tf_op jit(solution)/shard_map/all_to_all | solution.py:408
  47.7 0.7 %metrics.1 = f32[2,3]{1,0:T(2,128)} custom-call(f32[32,128]{1,0:T(8,128)S(1)} %bitcast.10), custom_call_target="tpu_custom_call" | custom-call | tf_op jit(solution)/shard_map/metrics/pallas_call | solution.py:409
  (9 shorter events, 0.1 us)
Async XLA Ops:
  0.6 36.2 %copy-start.1 = (f32[2,4096]{1,0:T(2,128)S(1)}, f32[2,4096]{1,0:T(2,128)}, u32[]{:S(2)}) copy-start(f32[2,4096]{1,0:T(2,128)} %dual_ref.1) | copy-start | bytes 98308
  0.6 36.2 %copy-start = (f32[2,4096]{1,0:T(2,128)S(1)}, f32[2,4096]{1,0:T(2,128)}, u32[]{:S(2)}) copy-start(f32[2,4096]{1,0:T(2,128)} %primal_ref.1) | copy-start | bytes 98308
  0.7 7.9 %collective-permute-start.4 = (f32[2,4096]{1,0:T(2,128)}, f32[2,4096]{1,0:T(2,128)S(1)}, u32[]{:S(2)}, u32[]{:S(2)}) collective-permute-start(f32[2,4096]{1,0:T(2,128)} %dual_ref.1), channel_id=1, source_target_pairs={{0,3},{1,2},{2,1},{3,0},{4,7},{5,6},{6,5},{7,4},{8,11},{9,10},{10,... | collective-permute-start | bytes 98312 | tf_op jit(solution)/shard_map/ppermute | solution.py:20
  3.1 6.0 %collective-permute-start.1 = (f32[2,4096]{1,0:T(2,128)}, f32[2,4096]{1,0:T(2,128)S(1)}, u32[]{:S(2)}, u32[]{:S(2)}) collective-permute-start(f32[2,4096]{1,0:T(2,128)} %primal_ref.1), channel_id=1, source_target_pairs={{0,16},{8,24},{16,0},{24,8},{1,17},{9,25},{17,1},{25,9},{2,18},{10... | collective-permute-start | bytes 98312 | tf_op jit(solution)/shard_map/ppermute | solution.py:20
  5.7 4.1 %collective-permute-start = (f32[2,4096]{1,0:T(2,128)}, f32[2,4096]{1,0:T(2,128)S(1)}, u32[]{:S(2)}, u32[]{:S(2)}) collective-permute-start(f32[2,4096]{1,0:T(2,128)} %primal_ref.1), channel_id=1, source_target_pairs={{0,8},{8,0},{16,24},{24,16},{1,9},{9,1},{17,25},{25,17},{2,10},{10... | collective-permute-start | bytes 98312 | tf_op jit(solution)/shard_map/ppermute | solution.py:20
  7.3 3.6 %collective-permute-start.6 = (f32[2,4096]{1,0:T(2,128)}, f32[2,4096]{1,0:T(2,128)S(1)}, u32[]{:S(2)}, u32[]{:S(2)}) collective-permute-start(f32[2,4096]{1,0:T(2,128)} %dual_ref.1), channel_id=1, source_target_pairs={{0,5},{1,4},{2,7},{3,6},{4,1},{5,0},{6,3},{7,2},{8,13},{9,12},{10,... | collective-permute-start | bytes 98312 | tf_op jit(solution)/shard_map/ppermute | solution.py:20
  8.5 3.3 %collective-permute-start.8 = (f32[2,4096]{1,0:T(2,128)S(1)}, f32[2,4096]{1,0:T(2,128)S(1)}, u32[]{:S(2)}, u32[]{:S(2)}) collective-permute-start(f32[2,4096]{1,0:T(2,128)S(1)} %collective-permute-done.4.refs_7_), channel_id=1, source_target_pairs={{0,5},{1,4},{2,7},{3,6},{4,1},{5,0},{6,3},{7,2},{8,13},{9,12},{10,... | collective-permute-start | bytes 98312 | tf_op jit(solution)/shard_map/ppermute | solution.py:20
  9.0 3.9 %collective-permute-start.3 = (f32[2,4096]{1,0:T(2,128)}, f32[2,4096]{1,0:T(2,128)S(1)}, u32[]{:S(2)}, u32[]{:S(2)}) collective-permute-start(f32[2,4096]{1,0:T(2,128)} %dual_ref.1), channel_id=1, source_target_pairs={{0,1},{1,0},{2,3},{3,2},{4,5},{5,4},{6,7},{7,6},{8,9},{9,8},{10,11... | collective-permute-start | bytes 98312 | tf_op jit(solution)/shard_map/ppermute | solution.py:20
  9.2 5.5 %collective-permute-start.5 = (f32[2,4096]{1,0:T(2,128)S(1)}, f32[2,4096]{1,0:T(2,128)S(1)}, u32[]{:S(2)}, u32[]{:S(2)}) collective-permute-start(f32[2,4096]{1,0:T(2,128)S(1)} %collective-permute-done.4.refs_7_), channel_id=1, source_target_pairs={{0,1},{1,0},{2,3},{3,2},{4,5},{5,4},{6,7},{7,6},{8,9},{9,8},{10,11... | collective-permute-start | bytes 98312 | tf_op jit(solution)/shard_map/ppermute | solution.py:20
  9.8 4.8 %collective-permute-start.2 = (f32[2,4096]{1,0:T(2,128)S(1)}, f32[2,4096]{1,0:T(2,128)S(1)}, u32[]{:S(2)}, u32[]{:S(2)}) collective-permute-start(f32[2,4096]{1,0:T(2,128)S(1)} %collective-permute-done.refs_1_), channel_id=1, source_target_pairs={{0,16},{8,24},{16,0},{24,8},{1,17},{9,25},{17,1},{25,9},{2,18},{10... | collective-permute-start | bytes 98312 | tf_op jit(solution)/shard_map/ppermute | solution.py:20
  10.9 3.8 %collective-permute-start.7 = (f32[2,4096]{1,0:T(2,128)S(1)}, f32[2,4096]{1,0:T(2,128)S(1)}, u32[]{:S(2)}, u32[]{:S(2)}) collective-permute-start(f32[2,4096]{1,0:T(2,128)S(1)} %collective-permute-done.6.refs_9_), channel_id=1, source_target_pairs={{0,1},{1,0},{2,3},{3,2},{4,5},{5,4},{6,7},{7,6},{8,9},{9,8},{10,11... | collective-permute-start | bytes 98312 | tf_op jit(solution)/shard_map/ppermute | solution.py:20
  11.9 2.8 %collective-permute-start.9 = (f32[2,4096]{1,0:T(2,128)S(1)}, f32[2,4096]{1,0:T(2,128)S(1)}, u32[]{:S(2)}, u32[]{:S(2)}) collective-permute-start(f32[2,4096]{1,0:T(2,128)S(1)} %collective-permute-done.8.refs_10_), channel_id=1, source_target_pairs={{0,1},{1,0},{2,3},{3,2},{4,5},{5,4},{6,7},{7,6},{8,9},{9,8},{10,11... | collective-permute-start | bytes 98312 | tf_op jit(solution)/shard_map/ppermute | solution.py:20
  27.4 1.4 %collective-permute-start.10 = (f32[4,2,32,128]{3,2,1,0:T(8,128)S(1)}, f32[4,2,32,128]{3,2,1,0:T(8,128)S(1)}, u32[]{:S(2)}, u32[]{:S(2)}) collective-permute-start(f32[4,2,32,128]{3,2,1,0:T(8,128)S(1)} %get-tuple-element.17), channel_id=1, source_target_pairs={{0,1},{1,0},{2,3},{3,2},{4,5},{5,4},{6,7},{7,6},{8,9},{9,8},{10,11... | collective-permute-start | bytes 393224 | tf_op jit(solution)/shard_map/ppermute | solution.py:20
  27.4 4.5 %collective-permute-start.13 = (f32[2,2,32,128]{3,2,1,0:T(8,128)S(1)}, f32[2,2,32,128]{3,2,1,0:T(8,128)S(1)}, u32[]{:S(2)}, u32[]{:S(2)}) collective-permute-start(f32[2,2,32,128]{3,2,1,0:T(8,128)S(1)} %get-tuple-element.19), channel_id=1, source_target_pairs={{0,8},{8,0},{16,24},{24,16},{1,9},{9,1},{17,25},{25,17},{2,10},{10... | collective-permute-start | bytes 196616 | tf_op jit(solution)/shard_map/ppermute | solution.py:20
  28.8 4.1 %collective-permute-start.11 = (f32[2,2,32,128]{3,2,1,0:T(8,128)S(1)}, f32[2,2,32,128]{3,2,1,0:T(8,128)S(1)}, u32[]{:S(2)}, u32[]{:S(2)}) collective-permute-start(f32[2,2,32,128]{3,2,1,0:T(8,128)S(1)} %get-tuple-element.30), channel_id=1, source_target_pairs={{0,3},{1,2},{2,1},{3,0},{4,7},{5,6},{6,5},{7,4},{8,11},{9,10},{10,... | collective-permute-start | bytes 196616 | tf_op jit(solution)/shard_map/ppermute | solution.py:20
  31.9 4.9 %collective-permute-start.14 = (f32[1,2,32,128]{3,2,1,0:T(8,128)S(1)}, f32[1,2,32,128]{3,2,1,0:T(8,128)S(1)}, u32[]{:S(2)}, u32[]{:S(2)}) collective-permute-start(f32[1,2,32,128]{3,2,1,0:T(8,128)S(1)} %get-tuple-element.31), channel_id=1, source_target_pairs={{0,16},{8,24},{16,0},{24,8},{1,17},{9,25},{17,1},{25,9},{2,18},{10... | collective-permute-start | bytes 98312 | tf_op jit(solution)/shard_map/ppermute | solution.py:20
  32.9 3.9 %collective-permute-start.12 = (f32[1,2,32,128]{3,2,1,0:T(8,128)S(1)}, f32[1,2,32,128]{3,2,1,0:T(8,128)S(1)}, u32[]{:S(2)}, u32[]{:S(2)}) collective-permute-start(f32[1,2,32,128]{3,2,1,0:T(8,128)S(1)} %get-tuple-element.33), channel_id=1, source_target_pairs={{0,5},{1,4},{2,7},{3,6},{4,1},{5,0},{6,3},{7,2},{8,13},{9,12},{10,... | collective-permute-start | bytes 98312 | tf_op jit(solution)/shard_map/ppermute | solution.py:20

commit v3 on v2

--- a/solution.py
+++ b/solution.py
@@ -63,7 +63,8 @@
     extra_in, refs = refs[:extras], refs[extras:]
     product_keep, product_send, transposed_keep, transposed_send = refs[:4]
     extra_out, refs = refs[4 : extras + 4], refs[extras + 4 :]
-    tiles, primal_ref, dual_ref, product, transposed, tile_sems, extra_sems = refs
+    tiles, primal_ref, dual_ref, product, transposed = refs[:5]
+    dual_lines, dual_columns, partial, tile_sems, extra_sems = refs[5:]
     my_row = lax.axis_index("row")
     my_col = lax.axis_index("col")
     live = count_ref[0, 0]
@@ -104,20 +105,25 @@
     row_blocks = row_share // block_size
     column_blocks = column_share // block_size
 
-    def one_tile(slot, carry):
+    def row_of(slot):
+        block_row = rows_ref[0, 0, slot]
+        return (block_row // row_blocks) ^ my_col, block_row % row_blocks
+
+    for slot in range(slot_count):
+        owner, inner = row_of(slot)
+        dual = dual_ref[owner, :, pl.ds(pl.multiple_of(inner * block_size, LANES), block_size)]
+        dual_lines[slot * candidates : (slot + 1) * candidates, :] = dual
+    for band in range(chunks):
+        span = slice(band * LANES, (band + 1) * LANES)
+        dual_columns[span, :] = dual_lines[:, span].T
+
+    def multiply(slot, carry):
         tile_copy(slot).wait()
-        block_row = rows_ref[0, 0, slot]
+        folding = fold(jnp.maximum(slot - 1, 0), slot > 0)
         block_column = columns_ref[0, 0, slot]
-        row_owner = (block_row // row_blocks) ^ my_col
-        column_owner = (block_column // column_blocks) ^ my_row
-        row_inner = block_row % row_blocks
-        column_inner = block_column % column_blocks
-        primal = primal_ref[
-            column_owner, :, pl.ds(pl.multiple_of(column_inner * block_size, LANES), block_size)
-        ]
-        dual = dual_ref[
-            row_owner, :, pl.ds(pl.multiple_of(row_inner * block_size, LANES), block_size)
-        ]
+        owner = (block_column // column_blocks) ^ my_row
+        inner = block_column % column_blocks
+        primal = primal_ref[owner, :, pl.ds(pl.multiple_of(inner * block_size, LANES), block_size)]
         spread = [
             [
                 jnp.broadcast_to(primal[s : s + 1, k * LANES : (k + 1) * LANES], (SUB, LANES))
@@ -125,44 +131,56 @@
             ]
             for s in range(candidates)
         ]
-        dual_rows = jnp.concatenate([dual, jnp.zeros((SUB - candidates, block_size), F32)], 0)
+        lanes = [jnp.full((SUB, LANES), slot * candidates + s, jnp.int32) for s in range(candidates)]
         sums = [[jnp.zeros((SUB, LANES), F32) for _ in range(chunks)] for _ in range(candidates)]
-        row_place = place_of(row_owner, bits_of(col_devices), True)
-        column_place = place_of(column_owner, bits_of(row_devices), False)
-        for band in range(chunks):
-            dual_column = dual_rows[:, band * LANES : (band + 1) * LANES].T
-            partial = [[] for _ in range(candidates)]
-            for group in range(LANES // SUB):
-                first = band * LANES + group * SUB
-                part = [
-                    tiles[slot, first : first + SUB, k * LANES : (k + 1) * LANES]
-                    for k in range(chunks)
-                ]
-                for s in range(candidates):
-                    weight = jnp.broadcast_to(
-                        dual_column[group * SUB : (group + 1) * SUB, s : s + 1], (SUB, LANES)
-                    )
-                    total = part[0] * spread[s][0]
-                    for k in range(1, chunks):
-                        total = total + part[k] * spread[s][k]
-                    partial[s].append(total)
-                    for k in range(chunks):
-                        sums[s][k] = sums[s][k] + part[k] * weight
+        for first in range(0, block_size, SUB):
+            if first % (block_size // 4) == 0:
+                next(folding, None)
+            part = [
+                tiles[slot, first : first + SUB, k * LANES : (k + 1) * LANES]
+                for k in range(chunks)
+            ]
+            column = dual_columns[first : first + SUB, :]
             for s in range(candidates):
-                turned = jnp.concatenate(partial[s], 0).T
-                values = jnp.sum(turned, axis=0, keepdims=True)
-                where = pl.ds(row_inner * chunks + band, 1)
-                product[row_place, s, where, :] = product[row_place, s, where, :] + values
+                weight = jnp.take_along_axis(column, lanes[s], axis=1)
+                total = part[0] * spread[s][0]
+                for k in range(1, chunks):
+                    total = total + part[k] * spread[s][k]
+                partial[slot, s, first : first + SUB, :] = total
+                for k in range(chunks):
+                    sums[s][k] = sums[s][k] + part[k] * weight
+        next(folding, None)
+        place = place_of(owner, bits_of(row_devices), False)
         for s in range(candidates):
             for k in range(chunks):
                 values = jnp.sum(sums[s][k], axis=0, keepdims=True)
-                where = pl.ds(column_inner * chunks + k, 1)
-                transposed[column_place, s, where, :] = (
-                    transposed[column_place, s, where, :] + values
-                )
+                where = pl.ds(inner * chunks + k, 1)
+                transposed[place, s, where, :] = transposed[place, s, where, :] + values
         return carry
 
-    lax.fori_loop(0, live, one_tile, 0)
+    def fold(slot, valid):
+        pieces = []
+        half = block_size // 2
+        for s in range(candidates):
+            for first in range(0, block_size, half):
+                whole = partial[slot, s, first : first + half, :]
+                high = whole.astype(jnp.bfloat16)
+                low = (whole - high.astype(F32)).astype(jnp.bfloat16)
+                pieces.append(sum_lanes(high) + sum_lanes(low))
+                yield
+        owner, inner = row_of(slot)
+        place = place_of(owner, bits_of(col_devices), True)
+        for s in range(candidates):
+            for band in range(chunks):
+                first = band * LANES
+                piece = pieces[s * 2 + first // half][:1, first % half : first % half + LANES]
+                values = jnp.where(valid, piece, 0.0)
+                where = pl.ds(inner * chunks + band, 1)
+                product[place, s, where, :] = product[place, s, where, :] + values
+
+    lax.fori_loop(0, live, multiply, 0)
+    for _ in fold(jnp.maximum(live - 1, 0), live > 0):
+        pass
     half = col_devices // 2
     product_keep[...] = product[:half]
     product_send[...] = product[half:]
@@ -171,6 +189,11 @@
     transposed_send[...] = transposed[half:]
     for copy in extra_copies:
         copy.wait()
+
+
+def sum_lanes(value):
+    ones = jnp.ones((SUB, value.shape[1]), value.dtype)
+    return lax.dot_general(ones, value, (((1,), (1,)), ((), ())), preferred_element_type=F32)
 
 
 def side_kernel(
@@ -354,6 +377,9 @@
             pltpu.VMEM((col_devices, candidates, row_share), F32),
             pltpu.VMEM(product_shape, F32),
             pltpu.VMEM(transposed_shape, F32),
+            pltpu.VMEM((LANES, block_size), F32),
+            pltpu.VMEM((block_size, LANES), F32),
+            pltpu.VMEM((slot_count, candidates, block_size, LANES), F32),
             pltpu.SemaphoreType.DMA((slot_count,)),
             pltpu.SemaphoreType.DMA((len(extras),)),
         ],

time: 48.9 us -> 44.7 us (0.914)
  Pallas kernels: 14.1 us -> 6.95 us
  starting transfers between devices: 11.8 us -> 18.4 us
  waiting for transfers between devices: 10.9 us -> 6.32 us
  blocking collectives: 10.2 us -> 10.8 us
    pallas_call x1, Pallas kernels: 12.7 us -> 5.56 us  [on_device(): pl.pallas_call(functools.partial(tile_kernel, slot_count=slot_count, bloc...]
    ppermute x15, starting transfers between devices: 11.8 us -> 18.4 us  [swap(): return lax.ppermute(value, axis, [(i, i ^ bit) for i in range(count)])]
    ppermute x15, waiting for transfers between devices: 10.9 us -> 6.32 us  [swap(): return lax.ppermute(value, axis, [(i, i ^ bit) for i in range(count)])]
    all_to_all x1, blocking collectives: 10.2 us -> 10.8 us  [on_device(): shared = lax.all_to_all(stats, ('row', 'col'), 0, 0)]
where the time goes in v3:
time: 44.7 us; the launch traced here: 43.9 us
  starting transfers between devices  18.4 us (41%)
  blocking collectives  10.8 us (24%)
  Pallas kernels  6.95 us (16%)
  waiting for transfers between devices  6.32 us (14%)
  between operations  1.35 us (3%)
    ppermute x15, starting transfers between devices, swap(): return lax.ppermute(value, axis, [(i, i ^ bit) for i in range(count)])  18.4 us
    all_to_all x1, blocking collectives, on_device(): shared = lax.all_to_all(stats, ('row', 'col'), 0, 0)  10.8 us
    ppermute x15, waiting for transfers between devices, swap(): return lax.ppermute(value, axis, [(i, i ^ bit) for i in range(count)])  6.32 us
    pallas_call x1, Pallas kernels, on_device(): pl.pallas_call(functools.partial(tile_kernel, slot_count=slot_count, bloc...  5.56 us
  transfers between devices with their start and end apart: 15, of which 7 were waited for; matrix products, arithmetic and copies ran while one was open for 0% of the time, Pallas kernels for 0%

profile of v3, /device:TPU:0, one launch (start us, length us, event | category | flops | bytes accessed | tf_op | source)
XLA Modules:
  0.0 43.9 jit_solution(2689930477783992362)
XLA Ops:
  0.7 2.5 %collective-permute-start.4 = (f32[2,4096]{1,0:T(2,128)}, f32[2,4096]{1,0:T(2,128)S(1)}, u32[]{:S(2)}, u32[]{:S(2)}) collective-permute-start(f32[2,4096]{1,0:T(2,128)} %dual_ref.1), channel_id=1, source_target_pairs={{0,3},{1,2},{2,1},{3,0},{4,7},{5,6},{6,5},{7,4},{8,11},{9,10},{10,... | collective-permute-start | bytes 98312 | tf_op jit(solution)/shard_map/ppermute | solution.py:20
  3.1 2.6 %collective-permute-start.1 = (f32[2,4096]{1,0:T(2,128)}, f32[2,4096]{1,0:T(2,128)S(1)}, u32[]{:S(2)}, u32[]{:S(2)}) collective-permute-start(f32[2,4096]{1,0:T(2,128)} %primal_ref.1), channel_id=1, source_target_pairs={{0,16},{8,24},{16,0},{24,8},{1,17},{9,25},{17,1},{25,9},{2,18},{10... | collective-permute-start | bytes 98312 | tf_op jit(solution)/shard_map/ppermute | solution.py:20
  5.7 1.6 %collective-permute-start = (f32[2,4096]{1,0:T(2,128)}, f32[2,4096]{1,0:T(2,128)S(1)}, u32[]{:S(2)}, u32[]{:S(2)}) collective-permute-start(f32[2,4096]{1,0:T(2,128)} %primal_ref.1), channel_id=1, source_target_pairs={{0,8},{8,0},{16,24},{24,16},{1,9},{9,1},{17,25},{25,17},{2,10},{10... | collective-permute-start | bytes 98312 | tf_op jit(solution)/shard_map/ppermute | solution.py:20
  7.3 1.2 %collective-permute-start.6 = (f32[2,4096]{1,0:T(2,128)}, f32[2,4096]{1,0:T(2,128)S(1)}, u32[]{:S(2)}, u32[]{:S(2)}) collective-permute-start(f32[2,4096]{1,0:T(2,128)} %dual_ref.1), channel_id=1, source_target_pairs={{0,5},{1,4},{2,7},{3,6},{4,1},{5,0},{6,3},{7,2},{8,13},{9,12},{10,... | collective-permute-start | bytes 98312 | tf_op jit(solution)/shard_map/ppermute | solution.py:20
  8.5 0.5 %collective-permute-start.8 = (f32[2,4096]{1,0:T(2,128)S(1)}, f32[2,4096]{1,0:T(2,128)S(1)}, u32[]{:S(2)}, u32[]{:S(2)}) collective-permute-start(f32[2,4096]{1,0:T(2,128)S(1)} %collective-permute-done.4.refs_7_), channel_id=1, source_target_pairs={{0,5},{1,4},{2,7},{3,6},{4,1},{5,0},{6,3},{7,2},{8,13},{9,12},{10,... | collective-permute-start | bytes 98312 | tf_op jit(solution)/shard_map/ppermute | solution.py:20
  9.0 0.1 collective-permute-start.3
  9.2 0.4 collective-permute-start.5
  9.6 0.3 collective-permute-done.refs_1_
  9.8 1.0 %collective-permute-start.2 = (f32[2,4096]{1,0:T(2,128)S(1)}, f32[2,4096]{1,0:T(2,128)S(1)}, u32[]{:S(2)}, u32[]{:S(2)}) collective-permute-start(f32[2,4096]{1,0:T(2,128)S(1)} %collective-permute-done.refs_1_), channel_id=1, source_target_pairs={{0,16},{8,24},{16,0},{24,8},{1,17},{9,25},{17,1},{25,9},{2,18},{10... | collective-permute-start | bytes 98312 | tf_op jit(solution)/shard_map/ppermute | solution.py:20
  10.9 0.0 collective-permute-done.6.refs_9_
  10.9 0.2 collective-permute-start.7
  11.1 0.8 %collective-permute-done.8.refs_10_ = f32[2,4096]{1,0:T(2,128)S(1)} collective-permute-done((f32[2,4096]{1,0:T(2,128)S(1)}, f32[2,4096]{1,0:T(2,128)S(1)}, u32[]{:S(2)}, u32[]{:S(2)}) %collective-permute-start.8) | collective-permute-done | bytes 32800 | tf_op jit(solution)/shard_map/ppermute | solution.py:20
  11.9 0.4 collective-permute-start.9
  12.9 0.0 collective-permute-done.3.refs_5_
  12.9 1.7 %collective-permute-done.2.refs_3_ = f32[2,4096]{1,0:T(2,128)S(1)} collective-permute-done((f32[2,4096]{1,0:T(2,128)S(1)}, f32[2,4096]{1,0:T(2,128)S(1)}, u32[]{:S(2)}, u32[]{:S(2)}) %collective-permute-start.2) | collective-permute-done | bytes 32800 | tf_op jit(solution)/shard_map/ppermute | solution.py:20
  14.7 0.0 collective-permute-done.7.refs_8_
  14.7 0.0 collective-permute-done.5.refs_6_
  14.7 0.0 collective-permute-done.9.refs_11_
  14.7 5.6 %tile_pass.1 = (f32[4,2,32,128]{3,2,1,0:T(8,128)S(1)}, f32[4,2,32,128]{3,2,1,0:T(8,128)S(1)}, f32[2,2,32,128]{3,2,1,0:T(8,128)S(1)}, f32[2,2,32,128]{3,2,1,0:T(8...) custom-call(s32[1,1,16]{2,1,0:T(1,128)} %rows_ref.1, ...), custom_call_target="tpu_custom_call" | custom-call | tf_op jit(solution)/shard_map/tile_pass/pallas_call | solution.py:351
  20.2 1.7 %collective-permute-start.10 = (f32[4,2,32,128]{3,2,1,0:T(8,128)S(1)}, f32[4,2,32,128]{3,2,1,0:T(8,128)S(1)}, u32[]{:S(2)}, u32[]{:S(2)}) collective-permute-start(f32[4,2,32,128]{3,2,1,0:T(8,128)S(1)} %get-tuple-element.17), channel_id=1, source_target_pairs={{0,1},{1,0},{2,3},{3,2},{4,5},{5,4},{6,7},{7,6},{8,9},{9,8},{10,11... | collective-permute-start | bytes 393224 | tf_op jit(solution)/shard_map/ppermute | solution.py:20
  22.0 0.7 %collective-permute-start.13 = (f32[2,2,32,128]{3,2,1,0:T(8,128)S(1)}, f32[2,2,32,128]{3,2,1,0:T(8,128)S(1)}, u32[]{:S(2)}, u32[]{:S(2)}) collective-permute-start(f32[2,2,32,128]{3,2,1,0:T(8,128)S(1)} %get-tuple-element.19), channel_id=1, source_target_pairs={{0,8},{8,0},{16,24},{24,16},{1,9},{9,1},{17,25},{25,17},{2,10},{10... | collective-permute-start | bytes 196616 | tf_op jit(solution)/shard_map/ppermute | solution.py:20
  22.7 0.3 collective-permute-done.10
  23.0 1.6 %collective-permute-start.11 = (f32[2,2,32,128]{3,2,1,0:T(8,128)S(1)}, f32[2,2,32,128]{3,2,1,0:T(8,128)S(1)}, u32[]{:S(2)}, u32[]{:S(2)}) collective-permute-start(f32[2,2,32,128]{3,2,1,0:T(8,128)S(1)} %get-tuple-element.30), channel_id=1, source_target_pairs={{0,3},{1,2},{2,1},{3,0},{4,7},{5,6},{6,5},{7,4},{8,11},{9,10},{10,... | collective-permute-start | bytes 196616 | tf_op jit(solution)/shard_map/ppermute | solution.py:20
  24.6 1.6 %collective-permute-done.13 = f32[2,2,32,128]{3,2,1,0:T(8,128)S(1)} collective-permute-done((f32[2,2,32,128]{3,2,1,0:T(8,128)S(1)}, f32[2,2,32,128]{3,2,1,0:T(8,128)S(1)}, u32[]{:S(2)}, u32[]{:S(2)}) %collective-permute-start.13) | collective-permute-done | bytes 65568 | tf_op jit(solution)/shard_map/ppermute | solution.py:20
  26.2 1.2 %collective-permute-start.14 = (f32[1,2,32,128]{3,2,1,0:T(8,128)S(1)}, f32[1,2,32,128]{3,2,1,0:T(8,128)S(1)}, u32[]{:S(2)}, u32[]{:S(2)}) collective-permute-start(f32[1,2,32,128]{3,2,1,0:T(8,128)S(1)} %get-tuple-element.31), channel_id=1, source_target_pairs={{0,16},{8,24},{16,0},{24,8},{1,17},{9,25},{17,1},{25,9},{2,18},{10... | collective-permute-start | bytes 98312 | tf_op jit(solution)/shard_map/ppermute | solution.py:20
  27.4 0.0 collective-permute-done.11
  27.5 2.6 %collective-permute-start.12 = (f32[1,2,32,128]{3,2,1,0:T(8,128)S(1)}, f32[1,2,32,128]{3,2,1,0:T(8,128)S(1)}, u32[]{:S(2)}, u32[]{:S(2)}) collective-permute-start(f32[1,2,32,128]{3,2,1,0:T(8,128)S(1)} %get-tuple-element.33), channel_id=1, source_target_pairs={{0,5},{1,4},{2,7},{3,6},{4,1},{5,0},{6,3},{7,2},{8,13},{9,12},{10,... | collective-permute-start | bytes 98312 | tf_op jit(solution)/shard_map/ppermute | solution.py:20
  30.1 1.1 %collective-permute-done.14.transposed_got = f32[1,2,32,128]{3,2,1,0:T(8,128)S(1)} collective-permute-done((f32[1,2,32,128]{3,2,1,0:T(8,128)S(1)}, f32[1,2,32,128]{3,2,1,0:T(8,128)S(1)}, u32[]{:S(2)}, u32[]{:S(2)}) %collective-permute-start.14) | collective-permute-done | bytes 32800 | tf_op jit(solution)/shard_map/ppermute | solution.py:20
  31.1 0.5 %collective-permute-done.12.product_got = f32[1,2,32,128]{3,2,1,0:T(8,128)S(1)} collective-permute-done((f32[1,2,32,128]{3,2,1,0:T(8,128)S(1)}, f32[1,2,32,128]{3,2,1,0:T(8,128)S(1)}, u32[]{:S(2)}, u32[]{:S(2)}) %collective-permute-start.12) | collective-permute-done | bytes 32800 | tf_op jit(solution)/shard_map/ppermute | solution.py:20
  31.7 0.7 %sides.1 = (f32[2,4096]{1,0:T(2,128)}, f32[2,4096]{1,0:T(2,128)}, f32[32,128]{1,0:T(8,128)S(1)}) custom-call(f32[1,2,32,128]{3,2,1,0:T(8,128)S(1)} %get-tuple-element.34.product_keep, f32[1,2,32,128]{3,2,1,0:T(8,128)S(1)} %collective-permute-done.12.product_got, f32[1,2,32,128]{3,2,1,0:T(8,128)S(1)} %get-tuple-element.32.transposed_keep, ...), custom_call_target="tpu_custom_call" | custom-call | tf_op jit(solution)/shard_map/sides/pallas_call | solution.py:414
  32.4 10.8 %all_to_all.11 = f32[32,1,128]{2,1,0:T(1,128)S(1)} all-to-all(f32[32,1,128]{2,1,0:T(1,128)S(1)} %bitcast.11), channel_id=1, replica_groups=mesh['row'=4,'col'=8] {'row','col'}, dimensions={0} | all-to-all | bytes 32768 | tf_op jit(solution)/shard_map/all_to_all | solution.py:434
  43.2 0.7 %metrics.1 = f32[2,3]{1,0:T(2,128)} custom-call(f32[32,128]{1,0:T(8,128)S(1)} %bitcast.10), custom_call_target="tpu_custom_call" | custom-call | tf_op jit(solution)/shard_map/metrics/pallas_call | solution.py:435
  (9 shorter events, 0.1 us)
Async XLA Ops:
  0.6 31.0 %copy-start.1 = (f32[2,4096]{1,0:T(2,128)S(1)}, f32[2,4096]{1,0:T(2,128)}, u32[]{:S(2)}) copy-start(f32[2,4096]{1,0:T(2,128)} %dual_ref.1) | copy-start | bytes 98308
  0.6 31.0 %copy-start = (f32[2,4096]{1,0:T(2,128)S(1)}, f32[2,4096]{1,0:T(2,128)}, u32[]{:S(2)}) copy-start(f32[2,4096]{1,0:T(2,128)} %primal_ref.1) | copy-start | bytes 98308
  0.7 7.9 %collective-permute-start.4 = (f32[2,4096]{1,0:T(2,128)}, f32[2,4096]{1,0:T(2,128)S(1)}, u32[]{:S(2)}, u32[]{:S(2)}) collective-permute-start(f32[2,4096]{1,0:T(2,128)} %dual_ref.1), channel_id=1, source_target_pairs={{0,3},{1,2},{2,1},{3,0},{4,7},{5,6},{6,5},{7,4},{8,11},{9,10},{10,... | collective-permute-start | bytes 98312 | tf_op jit(solution)/shard_map/ppermute | solution.py:20
  3.1 6.0 %collective-permute-start.1 = (f32[2,4096]{1,0:T(2,128)}, f32[2,4096]{1,0:T(2,128)S(1)}, u32[]{:S(2)}, u32[]{:S(2)}) collective-permute-start(f32[2,4096]{1,0:T(2,128)} %primal_ref.1), channel_id=1, source_target_pairs={{0,16},{8,24},{16,0},{24,8},{1,17},{9,25},{17,1},{25,9},{2,18},{10... | collective-permute-start | bytes 98312 | tf_op jit(solution)/shard_map/ppermute | solution.py:20
  5.7 4.1 %collective-permute-start = (f32[2,4096]{1,0:T(2,128)}, f32[2,4096]{1,0:T(2,128)S(1)}, u32[]{:S(2)}, u32[]{:S(2)}) collective-permute-start(f32[2,4096]{1,0:T(2,128)} %primal_ref.1), channel_id=1, source_target_pairs={{0,8},{8,0},{16,24},{24,16},{1,9},{9,1},{17,25},{25,17},{2,10},{10... | collective-permute-start | bytes 98312 | tf_op jit(solution)/shard_map/ppermute | solution.py:20
  7.3 3.6 %collective-permute-start.6 = (f32[2,4096]{1,0:T(2,128)}, f32[2,4096]{1,0:T(2,128)S(1)}, u32[]{:S(2)}, u32[]{:S(2)}) collective-permute-start(f32[2,4096]{1,0:T(2,128)} %dual_ref.1), channel_id=1, source_target_pairs={{0,5},{1,4},{2,7},{3,6},{4,1},{5,0},{6,3},{7,2},{8,13},{9,12},{10,... | collective-permute-start | bytes 98312 | tf_op jit(solution)/shard_map/ppermute | solution.py:20
  8.5 3.3 %collective-permute-start.8 = (f32[2,4096]{1,0:T(2,128)S(1)}, f32[2,4096]{1,0:T(2,128)S(1)}, u32[]{:S(2)}, u32[]{:S(2)}) collective-permute-start(f32[2,4096]{1,0:T(2,128)S(1)} %collective-permute-done.4.refs_7_), channel_id=1, source_target_pairs={{0,5},{1,4},{2,7},{3,6},{4,1},{5,0},{6,3},{7,2},{8,13},{9,12},{10,... | collective-permute-start | bytes 98312 | tf_op jit(solution)/shard_map/ppermute | solution.py:20
  9.0 3.9 %collective-permute-start.3 = (f32[2,4096]{1,0:T(2,128)}, f32[2,4096]{1,0:T(2,128)S(1)}, u32[]{:S(2)}, u32[]{:S(2)}) collective-permute-start(f32[2,4096]{1,0:T(2,128)} %dual_ref.1), channel_id=1, source_target_pairs={{0,1},{1,0},{2,3},{3,2},{4,5},{5,4},{6,7},{7,6},{8,9},{9,8},{10,11... | collective-permute-start | bytes 98312 | tf_op jit(solution)/shard_map/ppermute | solution.py:20
  9.2 5.5 %collective-permute-start.5 = (f32[2,4096]{1,0:T(2,128)S(1)}, f32[2,4096]{1,0:T(2,128)S(1)}, u32[]{:S(2)}, u32[]{:S(2)}) collective-permute-start(f32[2,4096]{1,0:T(2,128)S(1)} %collective-permute-done.4.refs_7_), channel_id=1, source_target_pairs={{0,1},{1,0},{2,3},{3,2},{4,5},{5,4},{6,7},{7,6},{8,9},{9,8},{10,11... | collective-permute-start | bytes 98312 | tf_op jit(solution)/shard_map/ppermute | solution.py:20
  9.8 4.8 %collective-permute-start.2 = (f32[2,4096]{1,0:T(2,128)S(1)}, f32[2,4096]{1,0:T(2,128)S(1)}, u32[]{:S(2)}, u32[]{:S(2)}) collective-permute-start(f32[2,4096]{1,0:T(2,128)S(1)} %collective-permute-done.refs_1_), channel_id=1, source_target_pairs={{0,16},{8,24},{16,0},{24,8},{1,17},{9,25},{17,1},{25,9},{2,18},{10... | collective-permute-start | bytes 98312 | tf_op jit(solution)/shard_map/ppermute | solution.py:20
  10.9 3.8 %collective-permute-start.7 = (f32[2,4096]{1,0:T(2,128)S(1)}, f32[2,4096]{1,0:T(2,128)S(1)}, u32[]{:S(2)}, u32[]{:S(2)}) collective-permute-start(f32[2,4096]{1,0:T(2,128)S(1)} %collective-permute-done.6.refs_9_), channel_id=1, source_target_pairs={{0,1},{1,0},{2,3},{3,2},{4,5},{5,4},{6,7},{7,6},{8,9},{9,8},{10,11... | collective-permute-start | bytes 98312 | tf_op jit(solution)/shard_map/ppermute | solution.py:20
  11.9 2.8 %collective-permute-start.9 = (f32[2,4096]{1,0:T(2,128)S(1)}, f32[2,4096]{1,0:T(2,128)S(1)}, u32[]{:S(2)}, u32[]{:S(2)}) collective-permute-start(f32[2,4096]{1,0:T(2,128)S(1)} %collective-permute-done.8.refs_10_), channel_id=1, source_target_pairs={{0,1},{1,0},{2,3},{3,2},{4,5},{5,4},{6,7},{7,6},{8,9},{9,8},{10,11... | collective-permute-start | bytes 98312 | tf_op jit(solution)/shard_map/ppermute | solution.py:20
  20.2 2.7 %collective-permute-start.10 = (f32[4,2,32,128]{3,2,1,0:T(8,128)S(1)}, f32[4,2,32,128]{3,2,1,0:T(8,128)S(1)}, u32[]{:S(2)}, u32[]{:S(2)}) collective-permute-start(f32[4,2,32,128]{3,2,1,0:T(8,128)S(1)} %get-tuple-element.17), channel_id=1, source_target_pairs={{0,1},{1,0},{2,3},{3,2},{4,5},{5,4},{6,7},{7,6},{8,9},{9,8},{10,11... | collective-permute-start | bytes 393224 | tf_op jit(solution)/shard_map/ppermute | solution.py:20
  22.0 4.3 %collective-permute-start.13 = (f32[2,2,32,128]{3,2,1,0:T(8,128)S(1)}, f32[2,2,32,128]{3,2,1,0:T(8,128)S(1)}, u32[]{:S(2)}, u32[]{:S(2)}) collective-permute-start(f32[2,2,32,128]{3,2,1,0:T(8,128)S(1)} %get-tuple-element.19), channel_id=1, source_target_pairs={{0,8},{8,0},{16,24},{24,16},{1,9},{9,1},{17,25},{25,17},{2,10},{10... | collective-permute-start | bytes 196616 | tf_op jit(solution)/shard_map/ppermute | solution.py:20
  23.0 4.5 %collective-permute-start.11 = (f32[2,2,32,128]{3,2,1,0:T(8,128)S(1)}, f32[2,2,32,128]{3,2,1,0:T(8,128)S(1)}, u32[]{:S(2)}, u32[]{:S(2)}) collective-permute-start(f32[2,2,32,128]{3,2,1,0:T(8,128)S(1)} %get-tuple-element.30), channel_id=1, source_target_pairs={{0,3},{1,2},{2,1},{3,0},{4,7},{5,6},{6,5},{7,4},{8,11},{9,10},{10,... | collective-permute-start | bytes 196616 | tf_op jit(solution)/shard_map/ppermute | solution.py:20
  26.2 4.9 %collective-permute-start.14 = (f32[1,2,32,128]{3,2,1,0:T(8,128)S(1)}, f32[1,2,32,128]{3,2,1,0:T(8,128)S(1)}, u32[]{:S(2)}, u32[]{:S(2)}) collective-permute-start(f32[1,2,32,128]{3,2,1,0:T(8,128)S(1)} %get-tuple-element.31), channel_id=1, source_target_pairs={{0,16},{8,24},{16,0},{24,8},{1,17},{9,25},{17,1},{25,9},{2,18},{10... | collective-permute-start | bytes 98312 | tf_op jit(solution)/shard_map/ppermute | solution.py:20
  27.5 4.2 %collective-permute-start.12 = (f32[1,2,32,128]{3,2,1,0:T(8,128)S(1)}, f32[1,2,32,128]{3,2,1,0:T(8,128)S(1)}, u32[]{:S(2)}, u32[]{:S(2)}) collective-permute-start(f32[1,2,32,128]{3,2,1,0:T(8,128)S(1)} %get-tuple-element.33), channel_id=1, source_target_pairs={{0,5},{1,4},{2,7},{3,6},{4,1},{5,0},{6,3},{7,2},{8,13},{9,12},{10,... | collective-permute-start | bytes 98312 | tf_op jit(solution)/shard_map/ppermute | solution.py:20

commit v4 on v3

--- a/solution.py
+++ b/solution.py
@@ -7,8 +7,10 @@
 from jax.experimental.pallas import tpu as pltpu
 from jax.sharding import PartitionSpec as P
 
+
 LANES = 128
 SUB = 8
+EARLY = 3
 F32 = jnp.float32
 
 
@@ -41,6 +43,33 @@
     for bit in range(1, bits):
         out = out | (((index >> bit) & 1) << (bits - 1 - bit))
     return out
+
+
+def stage_kernel(primal_in, dual_in, primal_out, dual_out, sems):
+    copies = [
+        pltpu.make_async_copy(primal_in, primal_out, sems.at[0]),
+        pltpu.make_async_copy(dual_in, dual_out, sems.at[1]),
+    ]
+    for copy in copies:
+        copy.start()
+    for copy in copies:
+        copy.wait()
+
+
+def early_kernel(tiles_ref, after_ref, out_ref, sems):
+    copies = [
+        pltpu.make_async_copy(tiles_ref.at[0, 0, slot], out_ref.at[slot], sems.at[slot])
+        for slot in range(out_ref.shape[0])
+    ]
+    for copy in copies:
+        copy.start()
+    for copy in copies:
+        copy.wait()
+
+
+def gather_step(mine, value, axis, bit, count):
+    got = swap(value, axis, bit, count)
+    return jnp.concatenate([mine, got], 0)
 
 
 def tile_kernel(
@@ -56,10 +85,11 @@
     row_share,
     column_share,
     extra_axes,
+    primal_order,
+    dual_order,
 ):
     extras = len(extra_axes)
-    primal_pieces, refs = refs[:row_devices], refs[row_devices:]
-    dual_pieces, refs = refs[:col_devices], refs[col_devices:]
+    (early_ref, primal_near, primal_far, dual_near, dual_far), refs = refs[:5], refs[5:]
     extra_in, refs = refs[:extras], refs[extras:]
     product_keep, product_send, transposed_keep, transposed_send = refs[:4]
     extra_out, refs = refs[4 : extras + 4], refs[extras + 4 :]
@@ -71,10 +101,13 @@
 
     def tile_copy(slot):
         return pltpu.make_async_copy(
-            tiles_ref.at[0, 0, slot], tiles.at[slot], tile_sems.at[slot]
+            tiles_ref.at[0, 0, slot],
+            tiles.at[slot - early],
+            tile_sems.at[slot - early],
         )
 
-    for slot in range(slot_count):
+    early = early_ref.shape[0]
+    for slot in range(early, slot_count):
 
         @pl.when(slot < live)
         def _():
@@ -94,10 +127,12 @@
         )
         extra_copies[-1].start()
 
-    for number, piece in enumerate(primal_pieces):
-        primal_ref[number] = piece[...]
-    for number, piece in enumerate(dual_pieces):
-        dual_ref[number] = piece[...]
+    for number, rel in enumerate(primal_order):
+        near = primal_near if number < primal_near.shape[0] else primal_far
+        primal_ref[rel] = near[number % primal_near.shape[0]]
+    for number, rel in enumerate(dual_order):
+        near = dual_near if number < dual_near.shape[0] else dual_far
+        dual_ref[rel] = near[number % dual_near.shape[0]]
     product[...] = jnp.zeros(product.shape, F32)
     transposed[...] = jnp.zeros(transposed.shape, F32)
     chunks = block_size // LANES
@@ -117,8 +152,16 @@
         span = slice(band * LANES, (band + 1) * LANES)
         dual_columns[span, :] = dual_lines[:, span].T
 
-    def multiply(slot, carry):
+    def multiply_early(slot, carry):
+        multiply(slot, slot, early_ref)
+        return carry
+
+    def multiply_late(slot, carry):
         tile_copy(slot).wait()
+        multiply(slot, slot - early, tiles)
+        return carry
+
+    def multiply(slot, place, source):
         folding = fold(jnp.maximum(slot - 1, 0), slot > 0)
         block_column = columns_ref[0, 0, slot]
         owner = (block_column // column_blocks) ^ my_row
@@ -137,7 +180,7 @@
             if first % (block_size // 4) == 0:
                 next(folding, None)
             part = [
-                tiles[slot, first : first + SUB, k * LANES : (k + 1) * LANES]
+                source[place, first : first + SUB, k * LANES : (k + 1) * LANES]
                 for k in range(chunks)
             ]
             column = dual_columns[first : first + SUB, :]
@@ -150,13 +193,12 @@
                 for k in range(chunks):
                     sums[s][k] = sums[s][k] + part[k] * weight
         next(folding, None)
-        place = place_of(owner, bits_of(row_devices), False)
+        turn = place_of(owner, bits_of(row_devices), False)
         for s in range(candidates):
             for k in range(chunks):
                 values = jnp.sum(sums[s][k], axis=0, keepdims=True)
                 where = pl.ds(inner * chunks + k, 1)
-                transposed[place, s, where, :] = transposed[place, s, where, :] + values
-        return carry
+                transposed[turn, s, where, :] = transposed[turn, s, where, :] + values
 
     def fold(slot, valid):
         pieces = []
@@ -178,7 +220,8 @@
                 where = pl.ds(inner * chunks + band, 1)
                 product[place, s, where, :] = product[place, s, where, :] + values
 
-    lax.fori_loop(0, live, multiply, 0)
+    lax.fori_loop(0, jnp.minimum(live, early), multiply_early, 0)
+    lax.fori_loop(early, jnp.maximum(live, early), multiply_late, 0)
     for _ in fold(jnp.maximum(live - 1, 0), live > 0):
         pass
     half = col_devices // 2
@@ -286,7 +329,7 @@
     out_ref[...] = jnp.concatenate(lines, 0)[:, : out_ref.shape[1]]
 
 
-def on_device(
+def restart_check(
     matrix_tiles,
     tile_rows,
     tile_columns,
@@ -307,27 +350,53 @@
     block_size = matrix_tiles.shape[-1]
     candidates, row_share = dual_iter.shape
     column_share = primal_iter.shape[1]
-    primal_pieces = {0: primal_iter}
-    dual_pieces = {0: dual_iter}
     row_steps = plain(row_devices)
     col_steps = crossed(col_devices)
+    smem = pl.BlockSpec(memory_space=pltpu.SMEM)
+    vmem = pl.BlockSpec(memory_space=pltpu.VMEM)
+    hbm = pl.BlockSpec(memory_space=pltpu.HBM)
+    primal_own, dual_own = pl.pallas_call(
+        stage_kernel,
+        name="stage",
+        in_specs=[hbm] * 2,
+        out_specs=[vmem] * 2,
+        out_shape=[
+            jax.ShapeDtypeStruct(primal_iter.shape, F32),
+            jax.ShapeDtypeStruct(dual_iter.shape, F32),
+        ],
+        scratch_shapes=[pltpu.SemaphoreType.DMA((2,))],
+        compiler_params=pltpu.CompilerParams(vmem_limit_bytes=4 << 20),
+    )(in_hbm(primal_iter), in_hbm(dual_iter))
+    primal_group, primal_send, primal_order = primal_own[None], primal_iter[None], [0]
+    dual_group, dual_send, dual_order = dual_own[None], dual_iter[None], [0]
+    gather_steps = col_steps[1:] + col_steps[:1]
     for step in range(max(len(row_steps), len(col_steps))):
-        if step < len(row_steps):
+        if step + 1 < len(row_steps):
             bit = row_steps[step]
-            primal_pieces.update(
-                {
-                    rel ^ bit: swap(value, "row", bit, row_devices)
-                    for rel, value in primal_pieces.items()
-                }
-            )
-        if step < len(col_steps):
-            bit = (col_steps[1:] + col_steps[:1])[step]
-            dual_pieces.update(
-                {
-                    rel ^ bit: swap(value, "col", bit, col_devices)
-                    for rel, value in dual_pieces.items()
-                }
-            )
+            primal_send = gather_step(primal_group, primal_send, "row", bit, row_devices)
+            primal_group, primal_order = primal_send, primal_order + [r ^ bit for r in primal_order]
+        elif step < len(row_steps):
+            bit = row_steps[step]
+            primal_far = swap(primal_group, "row", bit, row_devices)
+            primal_order = primal_order + [r ^ bit for r in primal_order]
+        if step + 1 < len(col_steps):
+            bit = gather_steps[step]
+            dual_send = gather_step(dual_group, dual_send, "col", bit, col_devices)
+            dual_group, dual_order = dual_send, dual_order + [r ^ bit for r in dual_order]
+        elif step < len(col_steps):
+            bit = gather_steps[step]
+            dual_far = swap(dual_group, "col", bit, col_devices)
+            dual_order = dual_order + [r ^ bit for r in dual_order]
+
+    early = pl.pallas_call(
+        early_kernel,
+        name="early_tiles",
+        in_specs=[hbm, vmem],
+        out_specs=vmem,
+        out_shape=jax.ShapeDtypeStruct((EARLY, block_size, block_size), F32),
+        scratch_shapes=[pltpu.SemaphoreType.DMA((EARLY,))],
+        compiler_params=pltpu.CompilerParams(vmem_limit_bytes=12 << 20),
+    )(in_hbm(matrix_tiles), dual_group)
 
     extras = (
         (requirement, "col", row_share),
@@ -337,9 +406,6 @@
         (upper_bound, "row", column_share),
         (variable_kind, "row", column_share),
     )
-    smem = pl.BlockSpec(memory_space=pltpu.SMEM)
-    vmem = pl.BlockSpec(memory_space=pltpu.VMEM)
-    hbm = pl.BlockSpec(memory_space=pltpu.HBM)
     row_height = row_share // LANES
     column_height = column_share // LANES
     product_shape = (col_devices, candidates, row_height, LANES)
@@ -358,11 +424,13 @@
             row_share=row_share,
             column_share=column_share,
             extra_axes=tuple(axis for _, axis, _ in extras),
+            primal_order=tuple(primal_order),
+            dual_order=tuple(dual_order),
         ),
         name="tile_pass",
         in_specs=[smem] * 3
         + [hbm]
-        + [vmem] * (row_devices + col_devices)
+        + [vmem] * 5
         + [hbm] * len(extras),
         out_specs=[vmem] * (4 + len(extras)),
         out_shape=[half_of(product_shape)] * 2
@@ -372,7 +440,7 @@
             for value, _, share in extras
         ],
         scratch_shapes=[
-            pltpu.VMEM((slot_count, block_size, block_size), F32),
+            pltpu.VMEM((slot_count - EARLY, block_size, block_size), F32),
             pltpu.VMEM((row_devices, candidates, column_share), F32),
             pltpu.VMEM((col_devices, candidates, row_share), F32),
             pltpu.VMEM(product_shape, F32),
@@ -380,7 +448,7 @@
             pltpu.VMEM((LANES, block_size), F32),
             pltpu.VMEM((block_size, LANES), F32),
             pltpu.VMEM((slot_count, candidates, block_size, LANES), F32),
-            pltpu.SemaphoreType.DMA((slot_count,)),
+            pltpu.SemaphoreType.DMA((slot_count - EARLY,)),
             pltpu.SemaphoreType.DMA((len(extras),)),
         ],
         compiler_params=pltpu.CompilerParams(vmem_limit_bytes=32 << 20),
@@ -389,10 +457,11 @@
         in_hbm(tile_columns),
         tile_counts,
         in_hbm(matrix_tiles),
-        in_hbm(primal_iter),
-        *[primal_pieces[rel] for rel in range(1, row_devices)],
-        in_hbm(dual_iter),
-        *[dual_pieces[rel] for rel in range(1, col_devices)],
+        early,
+        primal_group,
+        primal_far,
+        dual_group,
+        dual_far,
         *[in_hbm(value.reshape(-1, LANES)) for value, _, _ in extras],
     )
     product_keep, product_send, transposed_keep, transposed_send = outs[:4]
@@ -428,8 +497,8 @@
         transposed_keep,
         transposed_got,
         *outs[4:],
-        primal_iter,
-        dual_iter,
+        primal_own,
+        dual_own,
     )
     shared = lax.all_to_all(stats, ("row", "col"), 0, 0)
     metrics = pl.pallas_call(
@@ -460,7 +529,7 @@
     )
     return jax.shard_map(
         functools.partial(
-            on_device, row_devices=mesh.shape["row"], col_devices=mesh.shape["col"]
+            restart_check, row_devices=mesh.shape["row"], col_devices=mesh.shape["col"]
         ),
         mesh=mesh,
         in_specs=placed,

time: 44.7 us -> 48 us (1.074); the launches traced: 43.9 us -> 47.8 us
  starting transfers between devices: 18.4 us -> 13.4 us
  Pallas kernels: 6.95 us -> 10.9 us
  blocking collectives: 10.8 us -> 13.2 us
  waiting for transfers between devices: 6.32 us -> 8.71 us
    ppermute x15 -> x10, starting transfers between devices: 18.4 us -> 13.4 us  [swap(): return lax.ppermute(value, axis, [(i, i ^ bit) for i in range(count)])]
    pallas_call x3 -> x5, Pallas kernels: 6.95 us -> 10.9 us  [the longest x1 6.82 us: restart_check(): pl.pallas_call(functools.partial(tile_kernel, slot_count=slot_count, bloc...]
    all_to_all x1, blocking collectives: 10.8 us -> 13.2 us  [restart_check(): shared = lax.all_to_all(stats, ('row', 'col'), 0, 0)]
    ppermute x15 -> x10, waiting for transfers between devices: 6.32 us -> 8.71 us  [swap(): return lax.ppermute(value, axis, [(i, i ^ bit) for i in range(count)])]
  transfers between devices with their start and end apart: 15 -> 10, of which waited for: 7 -> 8; matrix products, arithmetic and copies ran while one was open for 0% -> 0% of each run, Pallas kernels for 0% -> 6%
where the time goes in v4:
time: 48 us; the launch traced here: 47.8 us
  starting transfers between devices  13.4 us (28%)
  blocking collectives  13.2 us (28%)
  Pallas kernels  10.9 us (23%)
  waiting for transfers between devices  8.71 us (18%)
  between operations  1.34 us (3%)
    ppermute x10, starting transfers between devices, swap(): return lax.ppermute(value, axis, [(i, i ^ bit) for i in range(count)])  13.4 us
    all_to_all x1, blocking collectives, restart_check(): shared = lax.all_to_all(stats, ('row', 'col'), 0, 0)  13.2 us
    ppermute x10, waiting for transfers between devices, swap(): return lax.ppermute(value, axis, [(i, i ^ bit) for i in range(count)])  8.71 us
    pallas_call x1, Pallas kernels, restart_check(): pl.pallas_call(functools.partial(tile_kernel, slot_count=slot_count, bloc...  6.82 us
    pallas_call x1, Pallas kernels, restart_check(): pl.pallas_call(early_kernel, name='early_tiles', in_specs=[hbm, vmem], ou...  1.89 us
  transfers between devices with their start and end apart: 10, of which 8 were waited for; matrix products, arithmetic and copies ran while one was open for 0% of the time, Pallas kernels for 6%

profile of v4, /device:TPU:0, one launch (start us, length us, event | category | flops | bytes accessed | tf_op | source)
XLA Modules:
  0.0 47.8 jit_solution(7480569924742467282)
XLA Ops:
  0.6 2.5 %collective-permute-start = (f32[1,2,4096]{2,1,0:T(2,128)}, f32[1,2,4096]{2,1,0:T(2,128)S(1)}, u32[]{:S(2)}, u32[]{:S(2)}) collective-permute-start(f32[1,2,4096]{2,1,0:T(2,128)} %bitcast.25), channel_id=1, source_target_pairs={{0,3},{1,2},{2,1},{3,0},{4,7},{5,6},{6,5},{7,4},{8,11},{9,10},{10,... | collective-permute-start | bytes 98312 | tf_op jit(solution)/shard_map/ppermute | solution.py:22
  3.1 0.8 %stage.1 = (f32[2,4096]{1,0:T(2,128)S(1)}, f32[2,4096]{1,0:T(2,128)S(1)}) custom-call(f32[2,4096]{1,0:T(2,128)} %primal_in.1, f32[2,4096]{1,0:T(2,128)} %dual_in.1), custom_call_target="tpu_custom_call" | custom-call | tf_op jit(solution)/shard_map/stage/pallas_call | solution.py:358
  3.9 1.3 %collective-permute-done = f32[1,2,4096]{2,1,0:T(2,128)S(1)} collective-permute-done((f32[1,2,4096]{2,1,0:T(2,128)}, f32[1,2,4096]{2,1,0:T(2,128)S(1)}, u32[]{:S(2)}, u32[]{:S(2)}) %collective-permute-start) | collective-permute-done | bytes 32800 | tf_op jit(solution)/shard_map/ppermute | solution.py:22
  5.2 2.1 %collective-permute-start.1 = (f32[2,2,4096]{2,1,0:T(2,128)S(1)}, f32[2,2,4096]{2,1,0:T(2,128)S(1)}, u32[]{:S(2)}, u32[]{:S(2)}) collective-permute-start(f32[2,2,4096]{2,1,0:T(2,128)S(1)} %pad_maximum_fusion.1), channel_id=1, source_target_pairs={{0,5},{1,4},{2,7},{3,6},{4,1},{5,0},{6,3},{7,2},{8,13},{9,12},{10,... | collective-permute-start | bytes 196616 | tf_op jit(solution)/shard_map/ppermute | solution.py:22
  7.4 1.6 %collective-permute-start.2 = (f32[1,2,4096]{2,1,0:T(2,128)}, f32[1,2,4096]{2,1,0:T(2,128)S(1)}, u32[]{:S(2)}, u32[]{:S(2)}) collective-permute-start(f32[1,2,4096]{2,1,0:T(2,128)} %bitcast.26), channel_id=1, source_target_pairs={{0,8},{8,0},{16,24},{24,16},{1,9},{9,1},{17,25},{25,17},{2,10},{10... | collective-permute-start | bytes 98312 | tf_op jit(solution)/shard_map/ppermute | solution.py:22
  8.9 0.6 %collective-permute-done.1 = f32[2,2,4096]{2,1,0:T(2,128)S(1)} collective-permute-done((f32[2,2,4096]{2,1,0:T(2,128)S(1)}, f32[2,2,4096]{2,1,0:T(2,128)S(1)}, u32[]{:S(2)}, u32[]{:S(2)}) %collective-permute-start.1) | collective-permute-done | bytes 65568 | tf_op jit(solution)/shard_map/ppermute | solution.py:22
  9.6 0.1 pad_maximum_fusion.after_ref.refs_3_
  9.6 0.3 collective-permute-start.4
  10.0 1.5 %collective-permute-done.2 = f32[1,2,4096]{2,1,0:T(2,128)S(1)} collective-permute-done((f32[1,2,4096]{2,1,0:T(2,128)}, f32[1,2,4096]{2,1,0:T(2,128)S(1)}, u32[]{:S(2)}, u32[]{:S(2)}) %collective-permute-start.2) | collective-permute-done | bytes 32800 | tf_op jit(solution)/shard_map/ppermute | solution.py:22
  11.5 2.7 %collective-permute-start.3 = (f32[2,2,4096]{2,1,0:T(2,128)S(1)}, f32[2,2,4096]{2,1,0:T(2,128)S(1)}, u32[]{:S(2)}, u32[]{:S(2)}) collective-permute-start(f32[2,2,4096]{2,1,0:T(2,128)S(1)} %pad_maximum_fusion.2.refs_1_), channel_id=1, source_target_pairs={{0,16},{8,24},{16,0},{24,8},{1,17},{9,25},{17,1},{25,9},{2,18},{10... | collective-permute-start | bytes 196616 | tf_op jit(solution)/shard_map/ppermute | solution.py:22
  14.8 1.9 %early_tiles.1.refs_0_ = f32[3,512,512]{2,1,0:T(8,128)S(1)} custom-call(f32[1,1,16,512,512]{4,3,2,1,0:T(8,128)} %tiles_ref.3, f32[4,2,4096]{2,1,0:T(2,128)S(1)} %pad_maximum_fusion.after_ref.refs_3_), custom_call_target="tpu_custom_call" | custom-call | tf_op jit(solution)/shard_map/early_tiles/pallas_call | solution.py:391
  16.7 0.2 collective-permute-done.3.refs_2_
  16.9 0.0 collective-permute-done.4.refs_4_
  16.9 6.8 %tile_pass.1 = (f32[4,2,32,128]{3,2,1,0:T(8,128)S(1)}, f32[4,2,32,128]{3,2,1,0:T(8,128)S(1)}, f32[2,2,32,128]{3,2,1,0:T(8,128)S(1)}, f32[2,2,32,128]{3,2,1,0:T(8...) custom-call(s32[1,1,16]{2,1,0:T(1,128)} %rows_ref.1, ...), custom_call_target="tpu_custom_call" | custom-call | tf_op jit(solution)/shard_map/tile_pass/pallas_call | solution.py:417
  23.7 0.1 collective-permute-start.5
  23.8 1.2 %collective-permute-start.8 = (f32[2,2,32,128]{3,2,1,0:T(8,128)S(1)}, f32[2,2,32,128]{3,2,1,0:T(8,128)S(1)}, u32[]{:S(2)}, u32[]{:S(2)}) collective-permute-start(f32[2,2,32,128]{3,2,1,0:T(8,128)S(1)} %get-tuple-element.23), channel_id=1, source_target_pairs={{0,8},{8,0},{16,24},{24,16},{1,9},{9,1},{17,25},{25,17},{2,10},{10... | collective-permute-start | bytes 196616 | tf_op jit(solution)/shard_map/ppermute | solution.py:22
  25.0 0.2 collective-permute-done.5
  25.1 0.1 collective-permute-start.6
  25.2 3.0 %collective-permute-done.8 = f32[2,2,32,128]{3,2,1,0:T(8,128)S(1)} collective-permute-done((f32[2,2,32,128]{3,2,1,0:T(8,128)S(1)}, f32[2,2,32,128]{3,2,1,0:T(8,128)S(1)}, u32[]{:S(2)}, u32[]{:S(2)}) %collective-permute-start.8) | collective-permute-done | bytes 65568 | tf_op jit(solution)/shard_map/ppermute | solution.py:22
  28.3 0.9 %collective-permute-start.9 = (f32[1,2,32,128]{3,2,1,0:T(8,128)S(1)}, f32[1,2,32,128]{3,2,1,0:T(8,128)S(1)}, u32[]{:S(2)}, u32[]{:S(2)}) collective-permute-start(f32[1,2,32,128]{3,2,1,0:T(8,128)S(1)} %get-tuple-element.35), channel_id=1, source_target_pairs={{0,16},{8,24},{16,0},{24,8},{1,17},{9,25},{17,1},{25,9},{2,18},{10... | collective-permute-start | bytes 98312 | tf_op jit(solution)/shard_map/ppermute | solution.py:22
  29.2 0.1 collective-permute-done.6
  29.3 2.0 %collective-permute-start.7 = (f32[1,2,32,128]{3,2,1,0:T(8,128)S(1)}, f32[1,2,32,128]{3,2,1,0:T(8,128)S(1)}, u32[]{:S(2)}, u32[]{:S(2)}) collective-permute-start(f32[1,2,32,128]{3,2,1,0:T(8,128)S(1)} %get-tuple-element.37), channel_id=1, source_target_pairs={{0,5},{1,4},{2,7},{3,6},{4,1},{5,0},{6,3},{7,2},{8,13},{9,12},{10,... | collective-permute-start | bytes 98312 | tf_op jit(solution)/shard_map/ppermute | solution.py:22
  31.3 1.9 %collective-permute-done.9.transposed_got = f32[1,2,32,128]{3,2,1,0:T(8,128)S(1)} collective-permute-done((f32[1,2,32,128]{3,2,1,0:T(8,128)S(1)}, f32[1,2,32,128]{3,2,1,0:T(8,128)S(1)}, u32[]{:S(2)}, u32[]{:S(2)}) %collective-permute-start.9) | collective-permute-done | bytes 32800 | tf_op jit(solution)/shard_map/ppermute | solution.py:22
  33.2 0.0 collective-permute-done.7.product_got
  33.2 0.7 %sides.1 = (f32[2,4096]{1,0:T(2,128)}, f32[2,4096]{1,0:T(2,128)}, f32[32,128]{1,0:T(8,128)S(1)}) custom-call(f32[1,2,32,128]{3,2,1,0:T(8,128)S(1)} %get-tuple-element.38.product_keep, f32[1,2,32,128]{3,2,1,0:T(8,128)S(1)} %collective-permute-done.7.product_got, f32[1,2,32,128]{3,2,1,0:T(8,128)S(1)} %get-tuple-element.36.transposed_keep, ...), custom_call_target="tpu_custom_call" | custom-call | tf_op jit(solution)/shard_map/sides/pallas_call | solution.py:483
  33.9 13.2 %all_to_all.11 = f32[32,1,128]{2,1,0:T(1,128)S(1)} all-to-all(f32[32,1,128]{2,1,0:T(1,128)S(1)} %bitcast.18), channel_id=1, replica_groups=mesh['row'=4,'col'=8] {'row','col'}, dimensions={0} | all-to-all | bytes 32768 | tf_op jit(solution)/shard_map/all_to_all | solution.py:503
  47.1 0.7 %metrics.1 = f32[2,3]{1,0:T(2,128)} custom-call(f32[32,128]{1,0:T(8,128)S(1)} %bitcast.17), custom_call_target="tpu_custom_call" | custom-call | tf_op jit(solution)/shard_map/metrics/pallas_call | solution.py:504
  (5 shorter events, 0.1 us)
Async XLA Ops:
  0.6 4.6 %collective-permute-start = (f32[1,2,4096]{2,1,0:T(2,128)}, f32[1,2,4096]{2,1,0:T(2,128)S(1)}, u32[]{:S(2)}, u32[]{:S(2)}) collective-permute-start(f32[1,2,4096]{2,1,0:T(2,128)} %bitcast.25), channel_id=1, source_target_pairs={{0,3},{1,2},{2,1},{3,0},{4,7},{5,6},{6,5},{7,4},{8,11},{9,10},{10,... | collective-permute-start | bytes 98312 | tf_op jit(solution)/shard_map/ppermute | solution.py:22
  5.2 4.3 %collective-permute-start.1 = (f32[2,2,4096]{2,1,0:T(2,128)S(1)}, f32[2,2,4096]{2,1,0:T(2,128)S(1)}, u32[]{:S(2)}, u32[]{:S(2)}) collective-permute-start(f32[2,2,4096]{2,1,0:T(2,128)S(1)} %pad_maximum_fusion.1), channel_id=1, source_target_pairs={{0,5},{1,4},{2,7},{3,6},{4,1},{5,0},{6,3},{7,2},{8,13},{9,12},{10,... | collective-permute-start | bytes 196616 | tf_op jit(solution)/shard_map/ppermute | solution.py:22
  7.4 4.1 %collective-permute-start.2 = (f32[1,2,4096]{2,1,0:T(2,128)}, f32[1,2,4096]{2,1,0:T(2,128)S(1)}, u32[]{:S(2)}, u32[]{:S(2)}) collective-permute-start(f32[1,2,4096]{2,1,0:T(2,128)} %bitcast.26), channel_id=1, source_target_pairs={{0,8},{8,0},{16,24},{24,16},{1,9},{9,1},{17,25},{25,17},{2,10},{10... | collective-permute-start | bytes 98312 | tf_op jit(solution)/shard_map/ppermute | solution.py:22
  9.6 7.3 %collective-permute-start.4 = (f32[4,2,4096]{2,1,0:T(2,128)S(1)}, f32[4,2,4096]{2,1,0:T(2,128)S(1)}, u32[]{:S(2)}, u32[]{:S(2)}) collective-permute-start(f32[4,2,4096]{2,1,0:T(2,128)S(1)} %pad_maximum_fusion.after_ref.refs_3_), channel_id=1, source_target_pairs={{0,1},{1,0},{2,3},{3,2},{4,5},{5,4},{6,7},{7,6},{8,9},{9,8},{10,11... | collective-permute-start | bytes 393224 | tf_op jit(solution)/shard_map/ppermute | solution.py:22
  11.5 5.4 %collective-permute-start.3 = (f32[2,2,4096]{2,1,0:T(2,128)S(1)}, f32[2,2,4096]{2,1,0:T(2,128)S(1)}, u32[]{:S(2)}, u32[]{:S(2)}) collective-permute-start(f32[2,2,4096]{2,1,0:T(2,128)S(1)} %pad_maximum_fusion.2.refs_1_), channel_id=1, source_target_pairs={{0,16},{8,24},{16,0},{24,8},{1,17},{9,25},{17,1},{25,9},{2,18},{10... | collective-permute-start | bytes 196616 | tf_op jit(solution)/shard_map/ppermute | solution.py:22
  23.7 1.4 %collective-permute-start.5 = (f32[4,2,32,128]{3,2,1,0:T(8,128)S(1)}, f32[4,2,32,128]{3,2,1,0:T(8,128)S(1)}, u32[]{:S(2)}, u32[]{:S(2)}) collective-permute-start(f32[4,2,32,128]{3,2,1,0:T(8,128)S(1)} %get-tuple-element.21), channel_id=1, source_target_pairs={{0,1},{1,0},{2,3},{3,2},{4,5},{5,4},{6,7},{7,6},{8,9},{9,8},{10,11... | collective-permute-start | bytes 393224 | tf_op jit(solution)/shard_map/ppermute | solution.py:22
  23.8 4.5 %collective-permute-start.8 = (f32[2,2,32,128]{3,2,1,0:T(8,128)S(1)}, f32[2,2,32,128]{3,2,1,0:T(8,128)S(1)}, u32[]{:S(2)}, u32[]{:S(2)}) collective-permute-start(f32[2,2,32,128]{3,2,1,0:T(8,128)S(1)} %get-tuple-element.23), channel_id=1, source_target_pairs={{0,8},{8,0},{16,24},{24,16},{1,9},{9,1},{17,25},{25,17},{2,10},{10... | collective-permute-start | bytes 196616 | tf_op jit(solution)/shard_map/ppermute | solution.py:22
  25.1 4.1 %collective-permute-start.6 = (f32[2,2,32,128]{3,2,1,0:T(8,128)S(1)}, f32[2,2,32,128]{3,2,1,0:T(8,128)S(1)}, u32[]{:S(2)}, u32[]{:S(2)}) collective-permute-start(f32[2,2,32,128]{3,2,1,0:T(8,128)S(1)} %get-tuple-element.34), channel_id=1, source_target_pairs={{0,3},{1,2},{2,1},{3,0},{4,7},{5,6},{6,5},{7,4},{8,11},{9,10},{10,... | collective-permute-start | bytes 196616 | tf_op jit(solution)/shard_map/ppermute | solution.py:22
  28.3 4.9 %collective-permute-start.9 = (f32[1,2,32,128]{3,2,1,0:T(8,128)S(1)}, f32[1,2,32,128]{3,2,1,0:T(8,128)S(1)}, u32[]{:S(2)}, u32[]{:S(2)}) collective-permute-start(f32[1,2,32,128]{3,2,1,0:T(8,128)S(1)} %get-tuple-element.35), channel_id=1, source_target_pairs={{0,16},{8,24},{16,0},{24,8},{1,17},{9,25},{17,1},{25,9},{2,18},{10... | collective-permute-start | bytes 98312 | tf_op jit(solution)/shard_map/ppermute | solution.py:22
  29.3 3.9 %collective-permute-start.7 = (f32[1,2,32,128]{3,2,1,0:T(8,128)S(1)}, f32[1,2,32,128]{3,2,1,0:T(8,128)S(1)}, u32[]{:S(2)}, u32[]{:S(2)}) collective-permute-start(f32[1,2,32,128]{3,2,1,0:T(8,128)S(1)} %get-tuple-element.37), channel_id=1, source_target_pairs={{0,5},{1,4},{2,7},{3,6},{4,1},{5,0},{6,3},{7,2},{8,13},{9,12},{10,... | collective-permute-start | bytes 98312 | tf_op jit(solution)/shard_map/ppermute | solution.py:22
